TPU v7x, 32 devices: a whole 2x2x4 slice. The times are simulated.
32 devices in a mesh: head: 2 (over y), view: 4 (over z), row: 4 (over x, core).
Axes of the slice: x: 2, y: 2, z: 4, core: 2. Of those that a mesh axis runs over, the one named last changes fastest.
Arguments:
- query_feats: bfloat16 [4, 32, 16, 1024], P('view', 'row', None, 'head'), may hold values from -125 to 125
- key_feats: bfloat16 [4, 32, 16, 1024], P('view', 'row', None, 'head'), may hold values from -7 to 7
- value_feats: bfloat16 [4, 32, 16, 1024], P('view', 'row', None, 'head'), may hold values from -6 to 6
- target: bfloat16 [4, 32, 16, 1024], P('view', 'row', None, 'head'), may hold values from -6 to 6
- token_rates: float32 [4, 2, 512], P('view', 'head', 'row'), may hold values from 5 to 100
- row_reach: int32 [32], P('row'), may hold values from 1 to 2
- view_counts: int32 [4], P('view'), may hold values from 170 to 512
- w_first: bfloat16 [2, 512, 512], P('head'), may hold values from -0.25 to 0.25
- w_third: bfloat16 [2, 512, 512], P('head'), may hold values from -0.25 to 0.25
- w_second: bfloat16 [2, 512, 512], P('head'), may hold values from -0.25 to 0.25
Outputs:
- fast_out: bfloat16 [4, 32, 16, 1024], P('view', 'row', None, 'head')
All inputs are finite; a program needn't handle non-finite values.
Results may differ from a plain program's by a relative error of at most 0.03.
Values may be sent and summed in bfloat16 or wider, within the bound.
A program may use at most 64 MiB of HBM per device.

v0:
```python
import functools
import math

import jax
import jax.numpy as jnp
from jax import lax
from jax.experimental import pallas as pl
from jax.experimental.pallas import tpu as pltpu
from jax.sharding import PartitionSpec as P

HD = 512
ATT_HD = 128
HALO = 2
MESH = pl.DeviceIdType.MESH
BF16 = jnp.bfloat16
F32 = jnp.float32
NT = (((1,), (1,)), ((), ()))
TN = (((0,), (0,)), ((), ()))


def with_halo(value, sides, width):
    for axis, dim in sides:
        size, length = (lax.axis_size(axis), value.shape[dim])
        up = [(i, (i + 1) % size) for i in range(size - 1)]
        down = [(j, i) for i, j in up]
        last = lax.slice_in_dim(value, length - width, length, axis=dim)
        leading = lax.slice_in_dim(value, 0, width, axis=dim)
        before = lax.ppermute(last, axis, up)
        after = lax.ppermute(leading, axis, down)
        value = jnp.concatenate([before, value, after], axis=dim)
    return value


def silu_slope(values_in):
    sigmoid_x = jax.nn.sigmoid(values_in)
    return sigmoid_x * (1.0 + values_in * (1.0 - sigmoid_x))


def attend(
    query_rows,
    key_rows,
    value_rows,
    q_row_ids,
    k_row_ids,
    q_tok,
    k_tok,
    k_valid,
    q_reach,
    grid_rows,
):
    count_q = query_rows.shape[0]
    count_k = key_rows.shape[0]
    groups = query_rows.shape[1] // ATT_HD
    query_heads = query_rows.reshape(count_q, groups, ATT_HD)
    key_heads = key_rows.reshape(count_k, groups, ATT_HD)
    value_heads = value_rows.reshape(count_k, groups, ATT_HD)
    scores = jnp.einsum(
        "qhd,khd->hqk", query_heads, key_heads, preferred_element_type=jnp.float32
    ) / math.sqrt(ATT_HD)
    inside = (k_row_ids >= 0) & (k_row_ids < grid_rows)
    in_band = jnp.abs(k_row_ids[None, :] - q_row_ids[:, None]) <= q_reach[:, None]
    allowed = in_band & inside[None, :] & (k_valid[None, :] | (k_tok[None, :] == q_tok[:, None]))
    scores = jnp.where(allowed[None], scores, -1e30)
    row_top = jnp.max(scores, -1, keepdims=True)
    powers = jnp.exp(scores - row_top)
    weights = (powers / jnp.sum(powers, -1, keepdims=True)).astype(jnp.bfloat16)
    output_rows = jnp.einsum(
        "hqk,khd->qhd", weights, value_heads, preferred_element_type=jnp.float32
    )
    return output_rows.reshape(count_q, groups * ATT_HD).astype(jnp.bfloat16)


def renorm(old_matrix, grad, total_valid):
    old_rows = old_matrix.astype(jnp.float32)
    raised = old_rows + grad / total_valid
    rescale = jnp.sqrt(jnp.sum(old_rows * old_rows, -1, keepdims=True) + 1e-06) / jnp.sqrt(
        jnp.sum(raised * raised, -1, keepdims=True) + 1e-06
    )
    return (raised * rescale).astype(jnp.bfloat16)


def per_device(
    query_feats,
    key_feats,
    value_feats,
    target,
    token_rates,
    row_reach,
    view_counts,
    w_first,
    w_third,
    w_second,
):
    row_count = query_feats.shape[1]
    col_count = query_feats.shape[2]
    feat_width = query_feats.shape[3]
    heads_here = feat_width // HD
    tokens_here = row_count * col_count
    key_span = row_count + 2 * HALO
    grid_rows = lax.axis_size("row") * row_count
    row_base = lax.axis_index("row") * row_count
    view_total = view_counts[0]
    total_valid = lax.psum(view_total.astype(jnp.float32), "view")
    paired = jnp.stack([key_feats[0], value_feats[0]], 0)
    padded = with_halo(paired, (("row", 1),), HALO)
    q_row_ids = row_base + jnp.repeat(jnp.arange(row_count, dtype=jnp.int32), col_count)
    k_row_ids = row_base - HALO + jnp.repeat(jnp.arange(key_span, dtype=jnp.int32), col_count)
    q_tok = q_row_ids * col_count + jnp.tile(jnp.arange(col_count, dtype=jnp.int32), row_count)
    k_tok = k_row_ids * col_count + jnp.tile(jnp.arange(col_count, dtype=jnp.int32), key_span)
    k_valid = k_tok < view_total
    q_reach = jnp.repeat(row_reach, col_count)
    attended = attend(
        query_feats[0].reshape(tokens_here, feat_width),
        padded[0].reshape(key_span * col_count, feat_width),
        padded[1].reshape(key_span * col_count, feat_width),
        q_row_ids,
        k_row_ids,
        q_tok,
        k_tok,
        k_valid,
        q_reach,
        grid_rows,
    )
    attended = attended.reshape(tokens_here, heads_here, HD).astype(jnp.float32)
    fast_keys = (
        attended * lax.rsqrt(jnp.mean(attended * attended, -1, keepdims=True) + 1e-06)
    ).astype(jnp.bfloat16)
    valid_mask = (q_tok < view_total).astype(jnp.float32)
    rates_tok = token_rates[0].T
    scaled = (
        rates_tok[:, :, None]
        * valid_mask[:, None, None]
        * target[0].reshape(tokens_here, heads_here, HD).astype(jnp.float32)
    ).astype(jnp.bfloat16)
    first_proj = jnp.einsum("thi,hij->thj", fast_keys, w_first, preferred_element_type=jnp.float32)
    third_proj = jnp.einsum("thi,hij->thj", fast_keys, w_third, preferred_element_type=jnp.float32)
    gated_rows = (jax.nn.silu(first_proj) * third_proj).astype(jnp.bfloat16)
    back_rows = jnp.einsum("tho,hjo->thj", scaled, w_second, preferred_element_type=jnp.float32)
    back_first = (back_rows * third_proj * silu_slope(first_proj)).astype(jnp.bfloat16)
    back_third = (back_rows * jax.nn.silu(first_proj)).astype(jnp.bfloat16)
    grad_first = jnp.einsum(
        "thi,thj->hij", fast_keys, back_first, preferred_element_type=jnp.float32
    )
    grad_third = jnp.einsum(
        "thi,thj->hij", fast_keys, back_third, preferred_element_type=jnp.float32
    )
    grad_second = jnp.einsum("thj,tho->hjo", gated_rows, scaled, preferred_element_type=jnp.float32)
    grad_first, grad_third, grad_second = lax.psum(
        (grad_first, grad_third, grad_second), ("view", "row")
    )
    new_first = renorm(w_first, grad_first, total_valid)
    new_third = renorm(w_third, grad_third, total_valid)
    new_second = renorm(w_second, grad_second, total_valid)
    applied = (
        jax.nn.silu(
            jnp.einsum("thi,hij->thj", fast_keys, new_first, preferred_element_type=jnp.float32)
        )
        * jnp.einsum("thi,hij->thj", fast_keys, new_third, preferred_element_type=jnp.float32)
    ).astype(jnp.bfloat16)
    fast_out = jnp.einsum(
        "thj,hjo->tho", applied, new_second, preferred_element_type=jnp.float32
    ).astype(jnp.bfloat16)
    return fast_out.reshape(1, row_count, col_count, feat_width)


def halve(values_in, size):
    if size & (size - 1) == 0:
        return values_in >> (size.bit_length() - 1)
    return lax.div(values_in, jnp.int32(size))


def dot(left, right, dims=(((1,), (0,)), ((), ()))):
    return lax.dot_general(left, right, dims, preferred_element_type=F32)


def flip(index, bits):
    bit = 1
    while bit <= bits:
        if bits & bit:
            index = index + bit - 2 * bit * lax.rem(lax.div(index, bit), 2)
        bit *= 2
    return index


def step_kernel(
    nr, nz, cols,
    q_hbm, k_hbm, v_hbm, t_hbm, rates_hbm, reach_hbm, count_hbm, wf_hbm, wt_hbm, ws_hbm,
    out_ref,
    q_ref, k_ref, v_ref, t_ref, rates_ref, reach_ref, count_ref, wf, wt, ws, halo, raw, kall, sall, cnt, gfull, gsend, grecv,
    wtr, news, ss, ssz, osend, orecv, load_sem, send_sem, recv_sem,
):
    tokens, width = q_ref.shape
    rows_here = tokens // cols
    hid = width // nr
    part = hid // nz
    edge = HALO * cols
    heads = width // ATT_HD
    me = lax.axis_index("row")
    mz = lax.axis_index("view")
    mine = pl.ds(pl.multiple_of(me * hid, hid), hid)
    here = pl.ds(pl.multiple_of(mz * part, part), part)

    def view_peer(bits):
        return flip(mz, bits)

    barrier = pltpu.get_barrier_semaphore()
    for d in range(1, nr):
        pl.semaphore_signal(barrier, inc=1, device_id={"row": flip(me, d)}, device_id_type=MESH)
    for d in range(1, nz):
        pl.semaphore_signal(barrier, inc=1, device_id={"view": view_peer(d)}, device_id_type=MESH)
    loads = [
        pltpu.make_async_copy(source, target, load_sem.at[i])
        for i, (source, target) in enumerate((
            (count_hbm, count_ref), (reach_hbm, reach_ref), (k_hbm, k_ref), (v_hbm, v_ref),
            (t_hbm, t_ref), (rates_hbm, rates_ref), (q_hbm, q_ref),
            (wf_hbm.at[:, mine], wf), (wt_hbm.at[:, mine], wt), (ws_hbm.at[mine, :], ws),
        ))
    ]
    for load in loads:
        load.start()

    used = [0]

    def send(source, target, axis, peer):
        slot = used[0]
        used[0] += 1
        copy = pltpu.make_async_remote_copy(
            src_ref=source, dst_ref=target,
            send_sem=send_sem.at[slot], recv_sem=recv_sem.at[slot],
            device_id={axis: peer}, device_id_type=MESH,
        )
        copy.start()
        return copy

    straight = [1] + list(range(2, nr, 2))

    def spread(at):
        return {d: send(at(0), at(d), "row", flip(me, d)) for d in straight}

    def hand_on(at, copies):
        for d in range(2, nr, 2):
            copies[d].wait_recv()
            copies[d + 1] = send(at(d), at(d + 1), "row", flip(me, 1))

    def settle(copies):
        for d in copies:
            copies[d].wait_send()

    above = lax.rem(me + 1, nr)
    below = lax.rem(me + (nr - 1), nr)

    row_base = me * rows_here
    tok_base = me * tokens
    for load in loads[:2]:
        load.wait()
    view_total = count_ref[0]
    cnt[0] = jnp.full((8, 128), view_total, jnp.int32).astype(F32)
    sub = lax.broadcasted_iota(jnp.int32, (tokens, tokens), 0)
    lane = lax.broadcasted_iota(jnp.int32, (tokens, tokens), 1)
    tok_col = tok_base + lax.broadcasted_iota(jnp.int32, (tokens, 1), 0)
    valid_col = (tok_col < view_total).astype(F32)
    for load in loads[2:6]:
        load.wait()
    rate_col = jnp.sum(jnp.where(sub == lane, rates_ref[...], 0.0), axis=1, keepdims=True)
    sall[0] = (rate_col * valid_col * t_ref[...].astype(F32)).astype(BF16)

    def allowed(q_tok, k_tok):
        q_row = halve(q_tok, cols)
        k_row = halve(k_tok + edge, cols) - HALO
        reach = jnp.zeros(q_tok.shape, jnp.int32)
        for r in range(rows_here):
            reach = jnp.where(q_row == r, reach_ref[r], reach)
        k_abs = k_row + row_base
        return (
            (jnp.abs(k_row - q_row) <= reach)
            & (k_abs >= 0)
            & (k_abs < nr * rows_here)
            & ((k_tok + tok_base < view_total) | (k_tok == q_tok))
        )

    near_ok = allowed(sub, lane)
    far_q = lax.broadcasted_iota(jnp.int32, (tokens, 2 * edge), 0)
    far_k = lax.broadcasted_iota(jnp.int32, (tokens, 2 * edge), 1)
    far_ok = allowed(far_q, jnp.where(far_k < edge, far_k - edge, far_k - edge + tokens))
    root = 1.0 / math.sqrt(ATT_HD)
    spans = [slice(h * ATT_HD, (h + 1) * ATT_HD) for h in range(heads)]
    loads[6].wait()
    near = [
        jnp.where(near_ok, dot(q_ref[:, hs], k_ref[:, hs], NT) * root, -1e30) for hs in spans
    ]
    near_top = [jnp.max(scores, axis=-1, keepdims=True) for scores in near]

    pl.semaphore_wait(barrier, (nr - 1) + (nz - 1))

    halo_copies = []
    for i, ref in enumerate((k_ref, v_ref)):
        halo_copies.append(send(ref.at[pl.ds(tokens - edge, edge)], halo.at[i, pl.ds(0, edge)], "row", above))
        halo_copies.append(send(ref.at[pl.ds(0, edge)], halo.at[i, pl.ds(edge, edge)], "row", below))
    s_copies = spread(lambda d: sall.at[d])
    c_copies = [send(cnt.at[0], cnt.at[d], "view", view_peer(d)) for d in range(1, nz)]
    for load in loads[7:]:
        load.wait()
    wtr[0] = wf[...].astype(F32).T
    wtr[1] = wt[...].astype(F32).T
    wtr[2] = ws[...].astype(F32)
    for copy in halo_copies:
        copy.wait()
    k_copies = []
    for h, hs in enumerate(spans):
        far = jnp.where(far_ok, dot(q_ref[:, hs], halo[0, :, hs], NT) * root, -1e30)
        top = jnp.maximum(near_top[h], jnp.max(far, axis=-1, keepdims=True))
        near_pow = jnp.exp(near[h] - top)
        far_pow = jnp.exp(far - top)
        inverse = 1.0 / (
            jnp.sum(near_pow, axis=-1, keepdims=True) + jnp.sum(far_pow, axis=-1, keepdims=True)
        )
        piece = dot((near_pow * inverse).astype(BF16), v_ref[:, hs]) + dot(
            (far_pow * inverse).astype(BF16), halo[1, :, hs]
        )
        raw[0, h] = piece.astype(BF16)
        k_copies.append(spread(lambda d, h=h: raw.at[d, h]))
    hand_on(lambda d: sall.at[d], s_copies)

    def normalise(d):
        pieces = [raw[d, h].astype(F32) for h in range(heads)]
        total_sq = jnp.sum(pieces[0] * pieces[0], axis=-1, keepdims=True)
        for piece in pieces[1:]:
            total_sq = total_sq + jnp.sum(piece * piece, axis=-1, keepdims=True)
        norm = lax.rsqrt(total_sq * (1.0 / width) + 1e-06)
        for hs, piece in zip(spans, pieces):
            kall[d, :, hs] = (piece * norm).astype(BF16)

    def factors(d):
        normalise(d)
        first = dot(kall[d], wf[...])
        third = dot(kall[d], wt[...])
        back = dot(sall[d], ws[...], NT)
        sig = jax.nn.sigmoid(first)
        gate = first * sig
        return (
            ((back * third * (sig * (1.0 + first * (1.0 - sig)))).astype(BF16), kall),
            ((back * gate).astype(BF16), kall),
            ((gate * third).astype(BF16), sall),
        )

    order = [0] + straight + list(range(3, nr, 2))
    g_copies = []
    for d in order:
        if d == 2:
            for h in range(heads):
                hand_on(lambda e, h=h: raw.at[e, h], k_copies[h])
        if d % 2:
            for copies in k_copies + [s_copies]:
                copies[d].wait_recv()
        for m, (left, right) in enumerate(factors(d)):
            grad = dot(left, right[d], TN)
            if d:
                grad = gfull[m] + grad
            gfull[m] = grad
            if d == order[-1]:
                for z in range(nz):
                    gsend[z, m] = grad[z * part:(z + 1) * part].astype(BF16)
                for e in range(nz - 1, 0, -1):
                    g_copies.append(
                        send(gsend.at[view_peer(e), m], grecv.at[e - 1, m], "view", view_peer(e))
                    )
    ss[0, 2:3] = jnp.sum(wtr[0] * wtr[0], axis=0, keepdims=True)
    ss[0, 3:4] = jnp.sum(wtr[1] * wtr[1], axis=0, keepdims=True)
    for copy in c_copies:
        copy.wait()
    total_valid = cnt[0, 0:1, 0:1]
    for d in range(1, nz):
        total_valid = total_valid + cnt[d, 0:1, 0:1]

    w_copies = []
    for m in range(3):
        for copy in g_copies[m * (nz - 1):(m + 1) * (nz - 1)]:
            copy.wait()
        grad = gfull[m, here, :]
        for d in range(1, nz):
            grad = grad + grecv[d - 1, m].astype(F32)
        old = wtr[m, here, :]
        raised = old + grad / total_valid
        if m == 2:
            rescale = jnp.sqrt(jnp.sum(old * old, -1, keepdims=True) + 1e-06) / jnp.sqrt(
                jnp.sum(raised * raised, -1, keepdims=True) + 1e-06
            )
            raised = raised * rescale
        else:
            ss[0, m:m + 1] = jnp.sum(raised * raised, axis=0, keepdims=True)
        news[0, m] = raised.astype(BF16)
        for d in range(nz - 1, 0, -1):
            w_copies.append(send(news.at[0, m], news.at[d, m], "view", view_peer(d)))
        if m == 1:
            ss_copies = [send(ss.at[0], ss.at[d], "row", flip(me, d)) for d in range(1, nr)]
    for copy in ss_copies:
        copy.wait()
    strip_sums = ss[0]
    for d in range(1, nr):
        strip_sums = strip_sums + ss[d]
    ssz[0] = strip_sums[0:2]
    ssz_copies = [send(ssz.at[0], ssz.at[d], "view", view_peer(d)) for d in range(1, nz)]
    for copy in ssz_copies:
        copy.wait()
    new_sums = ssz[0]
    for d in range(1, nz):
        new_sums = new_sums + ssz[d]
    scales = jnp.sqrt(strip_sums[2:4] + 1e-06) / jnp.sqrt(new_sums + 1e-06)

    for copy in w_copies:
        copy.wait()
    new_first, new_third, new_second = (
        jnp.concatenate([news[d, m] for d in range(nz)], axis=0) for m in range(3)
    )

    def share(d):
        keys = kall[d].astype(F32)
        first = dot((keys * scales[0:1]).astype(BF16), new_first, NT)
        third = dot((keys * scales[1:2]).astype(BF16), new_third, NT)
        return dot((first * jax.nn.sigmoid(first) * third).astype(BF16), new_second)

    o_copies = {}
    for d in list(range(3, nr, 2)) + list(range(2, nr, 2)) + [1, 0]:
        total = share(d)
        if d == 0:
            continue
        if d % 2 == 0:
            o_copies[d + 1].wait_recv()
            total = total + orecv[d].astype(F32)
        osend[d - 1] = total.astype(BF16)
        o_copies[d] = send(
            osend.at[d - 1], orecv.at[d - 1], "row", flip(me, 1) if d % 2 else flip(me, d)
        )
    for d in [1] + list(range(2, nr, 2)):
        o_copies[d].wait_recv()
        total = total + orecv[d - 1].astype(F32)
    out_ref[...] = total.astype(BF16)
    for copies in k_copies + [s_copies, o_copies]:
        settle(copies)


def fused_step(
    nr, nz,
    query_feats, key_feats, value_feats, target, token_rates, row_reach, view_counts,
    w_first, w_third, w_second,
):
    _, row_count, cols, width = query_feats.shape
    tokens = row_count * cols
    hid = width // nr
    part = hid // nz
    edge = HALO * cols
    heads = width // ATT_HD
    copies = 4 + (3 + heads) * (nr - 1) + 8 * (nz - 1)
    anywhere = pl.BlockSpec(memory_space=pl.ANY)
    flat = lambda a: a.reshape(tokens, width)
    out = pl.pallas_call(
        functools.partial(step_kernel, nr, nz, cols),
        out_shape=pltpu.VMEM((tokens, width), BF16),
        in_specs=[anywhere] * 5 + [pl.BlockSpec(memory_space=pltpu.HBM)] * 2 + [anywhere] * 3,
        out_specs=pl.BlockSpec(memory_space=pltpu.VMEM),
        scratch_shapes=[
            pltpu.VMEM((tokens, width), BF16),
            pltpu.VMEM((tokens, width), BF16),
            pltpu.VMEM((tokens, width), BF16),
            pltpu.VMEM((tokens, width), BF16),
            pltpu.VMEM((1, tokens), F32),
            pltpu.SMEM((row_count,), jnp.int32),
            pltpu.SMEM((1,), jnp.int32),
            pltpu.VMEM((width, hid), BF16),
            pltpu.VMEM((width, hid), BF16),
            pltpu.VMEM((hid, width), BF16),
            pltpu.VMEM((2, 2 * edge, width), BF16),
            pltpu.VMEM((nr, heads, tokens, ATT_HD), BF16),
            pltpu.VMEM((nr, tokens, width), BF16),
            pltpu.VMEM((nr, tokens, width), BF16),
            pltpu.VMEM((nz, 8, 128), F32),
            pltpu.VMEM((3, hid, width), F32),
            pltpu.VMEM((nz, 3, part, width), BF16),
            pltpu.VMEM((nz - 1, 3, part, width), BF16),
            pltpu.VMEM((3, hid, width), F32),
            pltpu.VMEM((nz, 3, part, width), BF16),
            pltpu.VMEM((nr, 4, width), F32),
            pltpu.VMEM((nz, 2, width), F32),
            pltpu.VMEM((nr - 1, tokens, width), BF16),
            pltpu.VMEM((nr - 1, tokens, width), BF16),
            pltpu.SemaphoreType.DMA((10,)),
            pltpu.SemaphoreType.DMA((copies,)),
            pltpu.SemaphoreType.DMA((copies,)),
        ],
        compiler_params=pltpu.CompilerParams(collective_id=0, has_side_effects=True),
    )(
        flat(query_feats), flat(key_feats), flat(value_feats), flat(target),
        token_rates.reshape(1, tokens), row_reach, view_counts,
        w_first.reshape(width, width), w_third.reshape(width, width), w_second.reshape(width, width),
    )
    return out.reshape(query_feats.shape)


def solution(mesh):
    placed = (
        P("view", "row", None, "head"),
        P("view", "row", None, "head"),
        P("view", "row", None, "head"),
        P("view", "row", None, "head"),
        P("view", "head", "row"),
        P("row"),
        P("view"),
        P("head", None, None),
        P("head", None, None),
        P("head", None, None),
    )
    nr, nz = mesh.shape["row"], mesh.shape["view"]
    pairs = nr > 1 and nr & (nr - 1) == 0
    fits = pairs and nz > 1 and nz & (nz - 1) == 0 and HD % (128 * nr) == 0 and HD % (16 * nr * nz) == 0
    return jax.shard_map(
        functools.partial(fused_step, nr, nz) if fits else per_device,
        mesh=mesh,
        in_specs=placed,
        out_specs=P("view", "row", None, "head"),
        check_vma=False,
    )
```

profile of v0, /device:TPU:1, one launch (start us, length us, event | category | flops | bytes accessed | tf_op | source)
XLA Modules:
  0.0 41.8 jit_solution(3961916054291397519)
XLA Ops:
  0.7 40.5 %shard_map.100 = bf16[128,512]{1,0:T(8,128)(2,1)S(1)} custom-call(bf16[128,512]{1,0:T(8,128)(2,1)} %bitcast.13, bf16[128,512]{1,0:T(8,128)(2,1)} %bitcast.14, bf16[128,512]{1,0:T(8,128)(2,1)} %bitcast.15, bf16[128,512]{1,0:T(8,128)(2,1)} %bitcast.16, f32[1,128]{1,0:T(1,128)} %bitcast.17, s32[8]{0:T(128)} %reach_hbm.1, s32[1]{0:T(128)S(6)} %copy.13.count_hbm, ...), custom_call_target="tpu_custom_call" | custom-call | tf_op jit(solution)/shard_map/pallas_call | solution.py:456
  41.1 0.7 %copy.12 = bf16[1,8,16,512]{3,2,1,0:T(8,128)(2,1)} copy(bf16[1,8,16,512]{3,2,1,0:T(8,128)(2,1)S(1)} %bitcast.9) | data formatting | bytes 262144
where the time goes:
time: 42.3 us; the launch traced here: 41.8 us
  Pallas kernels  40.5 us (96%)
  local copies, waits for them, and re-layouts  0.66 us (2%)
  between operations  0.66 us (2%)
    pallas_call x1, Pallas kernels, fused_step(): pl.pallas_call(functools.partial(step_kernel, nr, nz, cols), out_shape=pl...  40.5 us

commit v1 on v0

v1 whole, which is shorter than its diff:
```python
import functools
import math

import jax
import jax.numpy as jnp
from jax import lax
from jax.experimental import pallas as pl
from jax.experimental.pallas import tpu as pltpu
from jax.sharding import PartitionSpec as P

HD = 512
ATT_HD = 128
HALO = 2
PER = 4
MESH = pl.DeviceIdType.MESH
BF16 = jnp.bfloat16
F32 = jnp.float32
NT = (((1,), (1,)), ((), ()))
TN = (((0,), (0,)), ((), ()))


def with_halo(value, sides, width):
    for axis, dim in sides:
        size, length = (lax.axis_size(axis), value.shape[dim])
        up = [(i, (i + 1) % size) for i in range(size - 1)]
        down = [(j, i) for i, j in up]
        last = lax.slice_in_dim(value, length - width, length, axis=dim)
        leading = lax.slice_in_dim(value, 0, width, axis=dim)
        before = lax.ppermute(last, axis, up)
        after = lax.ppermute(leading, axis, down)
        value = jnp.concatenate([before, value, after], axis=dim)
    return value


def silu_slope(values_in):
    sigmoid_x = jax.nn.sigmoid(values_in)
    return sigmoid_x * (1.0 + values_in * (1.0 - sigmoid_x))


def attend(
    query_rows,
    key_rows,
    value_rows,
    q_row_ids,
    k_row_ids,
    q_tok,
    k_tok,
    k_valid,
    q_reach,
    grid_rows,
):
    count_q = query_rows.shape[0]
    count_k = key_rows.shape[0]
    groups = query_rows.shape[1] // ATT_HD
    query_heads = query_rows.reshape(count_q, groups, ATT_HD)
    key_heads = key_rows.reshape(count_k, groups, ATT_HD)
    value_heads = value_rows.reshape(count_k, groups, ATT_HD)
    scores = jnp.einsum(
        "qhd,khd->hqk", query_heads, key_heads, preferred_element_type=jnp.float32
    ) / math.sqrt(ATT_HD)
    inside = (k_row_ids >= 0) & (k_row_ids < grid_rows)
    in_band = jnp.abs(k_row_ids[None, :] - q_row_ids[:, None]) <= q_reach[:, None]
    allowed = in_band & inside[None, :] & (k_valid[None, :] | (k_tok[None, :] == q_tok[:, None]))
    scores = jnp.where(allowed[None], scores, -1e30)
    row_top = jnp.max(scores, -1, keepdims=True)
    powers = jnp.exp(scores - row_top)
    weights = (powers / jnp.sum(powers, -1, keepdims=True)).astype(jnp.bfloat16)
    output_rows = jnp.einsum(
        "hqk,khd->qhd", weights, value_heads, preferred_element_type=jnp.float32
    )
    return output_rows.reshape(count_q, groups * ATT_HD).astype(jnp.bfloat16)


def renorm(old_matrix, grad, total_valid):
    old_rows = old_matrix.astype(jnp.float32)
    raised = old_rows + grad / total_valid
    rescale = jnp.sqrt(jnp.sum(old_rows * old_rows, -1, keepdims=True) + 1e-06) / jnp.sqrt(
        jnp.sum(raised * raised, -1, keepdims=True) + 1e-06
    )
    return (raised * rescale).astype(jnp.bfloat16)


def per_device(
    query_feats,
    key_feats,
    value_feats,
    target,
    token_rates,
    row_reach,
    view_counts,
    w_first,
    w_third,
    w_second,
):
    row_count = query_feats.shape[1]
    col_count = query_feats.shape[2]
    feat_width = query_feats.shape[3]
    heads_here = feat_width // HD
    tokens_here = row_count * col_count
    key_span = row_count + 2 * HALO
    grid_rows = lax.axis_size("row") * row_count
    row_base = lax.axis_index("row") * row_count
    view_total = view_counts[0]
    total_valid = lax.psum(view_total.astype(jnp.float32), "view")
    paired = jnp.stack([key_feats[0], value_feats[0]], 0)
    padded = with_halo(paired, (("row", 1),), HALO)
    q_row_ids = row_base + jnp.repeat(jnp.arange(row_count, dtype=jnp.int32), col_count)
    k_row_ids = row_base - HALO + jnp.repeat(jnp.arange(key_span, dtype=jnp.int32), col_count)
    q_tok = q_row_ids * col_count + jnp.tile(jnp.arange(col_count, dtype=jnp.int32), row_count)
    k_tok = k_row_ids * col_count + jnp.tile(jnp.arange(col_count, dtype=jnp.int32), key_span)
    k_valid = k_tok < view_total
    q_reach = jnp.repeat(row_reach, col_count)
    attended = attend(
        query_feats[0].reshape(tokens_here, feat_width),
        padded[0].reshape(key_span * col_count, feat_width),
        padded[1].reshape(key_span * col_count, feat_width),
        q_row_ids,
        k_row_ids,
        q_tok,
        k_tok,
        k_valid,
        q_reach,
        grid_rows,
    )
    attended = attended.reshape(tokens_here, heads_here, HD).astype(jnp.float32)
    fast_keys = (
        attended * lax.rsqrt(jnp.mean(attended * attended, -1, keepdims=True) + 1e-06)
    ).astype(jnp.bfloat16)
    valid_mask = (q_tok < view_total).astype(jnp.float32)
    rates_tok = token_rates[0].T
    scaled = (
        rates_tok[:, :, None]
        * valid_mask[:, None, None]
        * target[0].reshape(tokens_here, heads_here, HD).astype(jnp.float32)
    ).astype(jnp.bfloat16)
    first_proj = jnp.einsum("thi,hij->thj", fast_keys, w_first, preferred_element_type=jnp.float32)
    third_proj = jnp.einsum("thi,hij->thj", fast_keys, w_third, preferred_element_type=jnp.float32)
    gated_rows = (jax.nn.silu(first_proj) * third_proj).astype(jnp.bfloat16)
    back_rows = jnp.einsum("tho,hjo->thj", scaled, w_second, preferred_element_type=jnp.float32)
    back_first = (back_rows * third_proj * silu_slope(first_proj)).astype(jnp.bfloat16)
    back_third = (back_rows * jax.nn.silu(first_proj)).astype(jnp.bfloat16)
    grad_first = jnp.einsum(
        "thi,thj->hij", fast_keys, back_first, preferred_element_type=jnp.float32
    )
    grad_third = jnp.einsum(
        "thi,thj->hij", fast_keys, back_third, preferred_element_type=jnp.float32
    )
    grad_second = jnp.einsum("thj,tho->hjo", gated_rows, scaled, preferred_element_type=jnp.float32)
    grad_first, grad_third, grad_second = lax.psum(
        (grad_first, grad_third, grad_second), ("view", "row")
    )
    new_first = renorm(w_first, grad_first, total_valid)
    new_third = renorm(w_third, grad_third, total_valid)
    new_second = renorm(w_second, grad_second, total_valid)
    applied = (
        jax.nn.silu(
            jnp.einsum("thi,hij->thj", fast_keys, new_first, preferred_element_type=jnp.float32)
        )
        * jnp.einsum("thi,hij->thj", fast_keys, new_third, preferred_element_type=jnp.float32)
    ).astype(jnp.bfloat16)
    fast_out = jnp.einsum(
        "thj,hjo->tho", applied, new_second, preferred_element_type=jnp.float32
    ).astype(jnp.bfloat16)
    return fast_out.reshape(1, row_count, col_count, feat_width)


def halve(values_in, size):
    if size & (size - 1) == 0:
        return values_in >> (size.bit_length() - 1)
    return lax.div(values_in, jnp.int32(size))


def dot(left, right, dims=(((1,), (0,)), ((), ()))):
    return lax.dot_general(left, right, dims, preferred_element_type=F32)


def flip(index, bits):
    bit = 1
    while bit <= bits:
        if bits & bit:
            index = index + bit - 2 * bit * lax.rem(lax.div(index, bit), 2)
        bit *= 2
    return index


def step_kernel(
    nr, nz, cols,
    q_hbm, k_hbm, v_hbm, t_hbm, rates_hbm, reach_hbm, count_hbm, wf_hbm, wt_hbm, ws_hbm,
    out_ref,
    q_ref, kv_ref, t_ref, rates_ref, reach_ref, count_ref, wft, ws, halo, raw, sall, norms, cnt, gfull, gsum, gin, gtot,
    wold, wnew, ss, mixed, osend, orecv, load_sem, row_send, row_recv, k_recv, view_send, out_recv, total_recv,
):
    tokens, width = q_ref.shape
    rows_here = tokens // cols
    hid = width // nr
    edge = HALO * cols
    heads = width // ATT_HD
    pieces = total_recv.shape[0]
    piece = 3 * hid // pieces
    per = pieces // 3
    me = lax.axis_index("row")
    mz = lax.axis_index("view")
    mine = pl.ds(pl.multiple_of(me * hid, hid), hid)
    low = mz < nz // 2
    inner = jnp.where(low, mz + 1, mz - 1)
    outer = jnp.where(low, mz - 1, mz + 1)
    center = (mz > 0) & (mz < nz - 1)
    leaf = (mz == 0) | (mz == nz - 1)
    has_above = me < nr - 1
    has_below = me > 0

    barrier = pltpu.get_barrier_semaphore()
    for d in range(1, nr):
        pl.semaphore_signal(barrier, inc=1, device_id={"row": flip(me, d)}, device_id_type=MESH)
    pl.semaphore_signal(barrier, inc=1, device_id={"view": inner}, device_id_type=MESH)

    @pl.when(center)
    def _():
        pl.semaphore_signal(barrier, inc=1, device_id={"view": outer}, device_id_type=MESH)

    loads = [
        pltpu.make_async_copy(source, target, load_sem.at[i])
        for i, (source, target) in enumerate((
            (k_hbm, kv_ref.at[0]), (v_hbm, kv_ref.at[1]), (count_hbm, count_ref), (reach_hbm, reach_ref),
            (t_hbm, t_ref), (rates_hbm, rates_ref), (q_hbm, q_ref),
            (wf_hbm.at[:, mine], wft.at[:, pl.ds(0, hid)]), (wt_hbm.at[:, mine], wft.at[:, pl.ds(hid, hid)]),
            (ws_hbm.at[mine, :], ws),
        ))
    ]
    for load in loads:
        load.start()

    def remote(source, target, sends, receives, axis, peer):
        return pltpu.make_async_remote_copy(
            src_ref=source, dst_ref=target, send_sem=sends, recv_sem=receives,
            device_id={axis: peer}, device_id_type=MESH,
        )

    partner, across = flip(me, 1), flip(me, 2)
    above, below = me + 1, me - 1

    @pl.when(me == 0)
    def _():
        halo[:, :edge] = jnp.zeros((2, edge, width), BF16)

    @pl.when(me == nr - 1)
    def _():
        halo[:, edge:] = jnp.zeros((2, edge, width), BF16)

    row_base = me * rows_here
    tok_base = me * tokens
    for load in loads[2:4]:
        load.wait()
    view_total = count_ref[0]
    cnt[0] = jnp.full((8, 128), view_total, jnp.int32).astype(F32)
    sub = lax.broadcasted_iota(jnp.int32, (tokens, tokens), 0)
    lane = lax.broadcasted_iota(jnp.int32, (tokens, tokens), 1)
    tok_col = tok_base + lax.broadcasted_iota(jnp.int32, (tokens, 1), 0)
    valid_col = (tok_col < view_total).astype(F32)
    for load in loads[4:6]:
        load.wait()
    rate_col = jnp.sum(jnp.where(sub == lane, rates_ref[...], 0.0), axis=1, keepdims=True)
    sall[0] = (rate_col * valid_col * t_ref[...].astype(F32)).astype(BF16)
    for load in loads[:2]:
        load.wait()

    pl.semaphore_wait(barrier, nr + jnp.where(center, 1, 0))

    up_halo = remote(kv_ref.at[:, pl.ds(tokens - edge, edge)], halo.at[:, pl.ds(0, edge)], row_send.at[0], row_recv.at[0], "row", above)
    down_halo = remote(kv_ref.at[:, pl.ds(0, edge)], halo.at[:, pl.ds(edge, edge)], row_send.at[1], row_recv.at[1], "row", below)

    @pl.when(has_above)
    def _():
        up_halo.start()

    @pl.when(has_below)
    def _():
        down_halo.start()

    s_near = remote(sall.at[0], sall.at[1], row_send.at[2], row_recv.at[2], "row", partner)
    s_far = remote(sall.at[0], sall.at[2], row_send.at[2], row_recv.at[3], "row", across)
    s_on = remote(sall.at[2], sall.at[3], row_send.at[2], row_recv.at[4], "row", partner)
    s_near.start()
    s_far.start()
    cnt_up = remote(cnt.at[0], cnt.at[1], view_send.at[0], row_recv.at[8], "view", inner)
    cnt_mid = remote(cnt.at[2], cnt.at[3], view_send.at[0], row_recv.at[9], "view", inner)
    cnt_down = remote(cnt.at[3], cnt.at[3], view_send.at[1], row_recv.at[9], "view", outer)

    @pl.when(leaf)
    def _():
        cnt_up.start()

    def allowed(q_tok, k_tok):
        q_row = halve(q_tok, cols)
        k_row = halve(k_tok + edge, cols) - HALO
        reach = jnp.zeros(q_tok.shape, jnp.int32)
        for r in range(rows_here):
            reach = jnp.where(q_row == r, reach_ref[r], reach)
        k_abs = k_row + row_base
        return (
            (jnp.abs(k_row - q_row) <= reach)
            & (k_abs >= 0)
            & (k_abs < nr * rows_here)
            & ((k_tok + tok_base < view_total) | (k_tok == q_tok))
        )

    near_ok = allowed(sub, lane)
    far_q = lax.broadcasted_iota(jnp.int32, (tokens, 2 * edge), 0)
    far_k = lax.broadcasted_iota(jnp.int32, (tokens, 2 * edge), 1)
    far_ok = allowed(far_q, jnp.where(far_k < edge, far_k - edge, far_k - edge + tokens))
    root = 1.0 / math.sqrt(ATT_HD)
    spans = [slice(h * ATT_HD, (h + 1) * ATT_HD) for h in range(heads)]
    loads[6].wait()
    near = []
    for hs in spans:
        scores = jnp.where(near_ok, dot(q_ref[:, hs], kv_ref[0, :, hs], NT) * root, -1e30)
        top = jnp.max(scores, axis=-1, keepdims=True)
        power = jnp.exp(scores - top)
        near.append((top, jnp.sum(power, axis=-1, keepdims=True), dot(power.astype(BF16), kv_ref[1, :, hs])))
    for load in loads[7:]:
        load.wait()
    wold[0:hid] = wft[:, :hid].astype(F32).T
    wold[hid:2 * hid] = wft[:, hid:].astype(F32).T
    wold[2 * hid:] = ws[...].astype(F32)

    @pl.when(has_below)
    def _():
        up_halo.wait_recv()

    @pl.when(has_above)
    def _():
        down_halo.wait_recv()

    k_near, k_far, k_on = [], [], []
    for h, hs in enumerate(spans):
        near_top, near_sum, near_out = near[h]
        far = jnp.where(far_ok, dot(q_ref[:, hs], halo[0, :, hs], NT) * root, -1e30)
        top = jnp.maximum(near_top, jnp.max(far, axis=-1, keepdims=True))
        power = jnp.exp(far - top)
        keep = jnp.exp(near_top - top)
        inverse = 1.0 / (keep * near_sum + jnp.sum(power, axis=-1, keepdims=True))
        mix = keep * near_out + dot(power.astype(BF16), halo[1, :, hs])
        raw[0, h] = (mix * inverse).astype(BF16)
        k_near.append(remote(raw.at[0, h], raw.at[1, h], row_send.at[3], k_recv.at[0, h], "row", partner))
        k_far.append(remote(raw.at[0, h], raw.at[2, h], row_send.at[3], k_recv.at[1, h], "row", across))
        k_on.append(remote(raw.at[2, h], raw.at[3, h], row_send.at[3], k_recv.at[2, h], "row", partner))
        k_far[h].start()
        k_near[h].start()

    def block(d):
        keys = jnp.concatenate([raw[d, h] for h in range(heads)], axis=1)
        both = dot(keys, wft[...])
        back = dot(sall[d], ws[...], NT)
        total_sq = jnp.zeros((tokens, ATT_HD), F32)
        for h in range(heads):
            part = raw[d, h].astype(F32)
            total_sq = total_sq + part * part
        norm = lax.rsqrt(jnp.sum(total_sq, axis=-1, keepdims=True) * (1.0 / width) + 1e-06)
        norms[d] = jnp.broadcast_to(norm, (tokens, 128))
        first = both[:, :hid] * norm
        third = both[:, hid:] * norm
        sig = jax.nn.sigmoid(first)
        gate = first * sig
        pulled = back * norm
        left = jnp.concatenate(
            [
                (pulled * third * (sig * (1.0 + first * (1.0 - sig)))).astype(BF16),
                (pulled * gate).astype(BF16),
            ],
            axis=1,
        )
        return left, keys, (gate * third).astype(BF16)

    def grads(d, first_block):
        left, keys, gated = block(d)
        grad = dot(left, keys, TN)
        gfull[: 2 * hid] = grad if first_block else gfull[: 2 * hid] + grad
        grad = dot(gated, sall[d], TN)
        gfull[2 * hid:] = grad if first_block else gfull[2 * hid:] + grad

    grads(0, True)
    s_near.wait_recv()
    for copy in k_near:
        copy.wait_recv()
    grads(1, False)

    @pl.when(center)
    def _():
        cnt_up.wait_recv()
        cnt[2] = cnt[0] + cnt[1]
        cnt_mid.start()

    s_far.wait_recv()
    s_on.start()
    for h in range(heads):
        k_far[h].wait_recv()
        k_on[h].start()
    grads(2, False)

    @pl.when(center)
    def _():
        cnt_mid.wait_recv()
        cnt[3] = cnt[2] + cnt[3]
        cnt_down.start()

    s_on.wait_recv()
    for copy in k_on:
        copy.wait_recv()

    def rows(i):
        return pl.ds(i * piece, piece)

    def rise(i, target, receives):
        return remote(gsum.at[rows(i)], target.at[rows(i)], view_send.at[2], receives.at[i], "view", inner)

    def fall(i):
        return remote(gtot.at[rows(i)], gtot.at[rows(i)], view_send.at[3], total_recv.at[i], "view", outer)

    left, keys, gated = block(3)
    grad = gfull[: 2 * hid] + dot(left, keys, TN)
    gfull[: 2 * hid] = grad

    @pl.when(leaf)
    def _():
        for i in range(2 * per):
            gsum[rows(i)] = gfull[rows(i)].astype(BF16)
            rise(i, gin, out_recv).start()

    grad = gfull[2 * hid:] + dot(gated, sall[3], TN)
    gfull[2 * hid:] = grad

    @pl.when(leaf)
    def _():
        for i in range(2 * per, 3 * per):
            gsum[rows(i)] = gfull[rows(i)].astype(BF16)
            rise(i, gin, out_recv).start()
        cnt_down.wait_recv()

    ss[0, 2:3] = jnp.sum(wold[:hid] * wold[:hid], axis=0, keepdims=True)
    ss[0, 3:4] = jnp.sum(wold[hid:2 * hid] * wold[hid:2 * hid], axis=0, keepdims=True)
    second_old = wold[2 * hid:]
    second_size = jnp.sqrt(jnp.sum(second_old * second_old, axis=-1, keepdims=True) + 1e-06)
    share_total = 1.0 / cnt[3, 0:1, 0:1]

    def join(i):
        rise(i, gin, out_recv).wait_recv()
        gsum[rows(i)] = (gfull[rows(i)] + gin[rows(i)].astype(F32)).astype(BF16)
        rise(i, gtot, total_recv).start()

    def finish(i):
        rise(i, gtot, total_recv).wait_recv()
        gtot[rows(i)] = (gsum[rows(i)].astype(F32) + gtot[rows(i)].astype(F32)).astype(BF16)
        fall(i).start()

    lag = 3

    @pl.when(center)
    def _():
        for i in range(lag):
            join(i)

    def arrive(i):
        @pl.when(center)
        def _():
            if i + lag < pieces:
                join(i + lag)
            finish(i)

    def land(i):
        @pl.when(leaf)
        def _():
            fall(i).wait_recv()

    def raise_rows(i):
        raised = wold[rows(i)] + gtot[rows(i)].astype(F32) * share_total
        if i < 2 * per:
            wnew[rows(i)] = raised
            return jnp.sum(raised * raised, axis=0, keepdims=True)
        at = (i - 2 * per) * piece
        size = jnp.sqrt(jnp.sum(raised * raised, axis=-1, keepdims=True) + 1e-06)
        ws[at:at + piece] = (raised * (second_size[at:at + piece] / size)).astype(BF16)

    ss_copies = [
        remote(ss.at[0], ss.at[d], row_send.at[3 + d], row_recv.at[4 + d], "row", flip(me, d)) for d in range(1, nr)
    ]
    for i in range(pieces):
        arrive(i)
        if i == pieces - 1:
            break
        land(i)
        square = raise_rows(i)
        if i < 2 * per:
            running = square if i % per == 0 else running + square
            if i % per == per - 1:
                m = i // per
                ss[0, m:m + 1] = running
                if m == 1:
                    for copy in ss_copies:
                        copy.start()
    for copy in ss_copies:
        copy.wait_recv()
    sums = ss[0]
    for d in range(1, nr):
        sums = sums + ss[d]
    scales = jnp.sqrt(sums[2:4] + 1e-06) / jnp.sqrt(sums[0:2] + 1e-06)
    mixed[:hid] = (wnew[:hid] * scales[0:1]).astype(BF16)
    mixed[hid:] = (wnew[hid:] * scales[1:2]).astype(BF16)
    order = list(range(3, nr, 2)) + list(range(2, nr, 2)) + [1, 0]
    applied = {}
    for d in order:
        keys = jnp.concatenate([raw[d, h] for h in range(heads)], axis=1)
        both = dot(keys, mixed[...], NT)
        first = both[:, :hid] * norms[d][:, 0:1]
        third = both[:, hid:] * norms[d][:, 0:1]
        applied[d] = (first * jax.nn.sigmoid(first) * third).astype(BF16)
    land(pieces - 1)
    raise_rows(pieces - 1)

    def leave(d, peer):
        return remote(osend.at[d - 1], orecv.at[d - 1], row_send.at[nr + 3], row_recv.at[9 + d], "row", peer)

    o_copies = {1: leave(1, partner), 2: leave(2, across), 3: leave(3, partner)}
    for d in order:
        total = dot(applied[d], ws[...])
        if d == 0:
            continue
        if d % 2 == 0:
            o_copies[d + 1].wait_recv()
            total = total + orecv[d].astype(F32)
        osend[d - 1] = total.astype(BF16)
        o_copies[d].start()
    for d in [1] + list(range(2, nr, 2)):
        o_copies[d].wait_recv()
        total = total + orecv[d - 1].astype(F32)
    out_ref[...] = total.astype(BF16)

    @pl.when(has_above)
    def _():
        up_halo.wait_send()

    @pl.when(has_below)
    def _():
        down_halo.wait_send()

    remote(sall.at[pl.ds(0, nr - 1)], sall.at[pl.ds(0, nr - 1)], row_send.at[2], row_recv.at[2], "row", partner).wait_send()
    remote(raw.at[pl.ds(0, nr - 1)], raw.at[pl.ds(0, nr - 1)], row_send.at[3], row_recv.at[2], "row", partner).wait_send()
    remote(osend, orecv, row_send.at[nr + 3], row_recv.at[2], "row", partner).wait_send()
    for copy in ss_copies:
        copy.wait_send()
    remote(gsum, gin, view_send.at[2], row_recv.at[2], "view", inner).wait_send()
    cnt_up.wait_send()

    @pl.when(center)
    def _():
        cnt_down.wait_send()
        remote(gtot, gtot, view_send.at[3], row_recv.at[2], "view", outer).wait_send()


def fused_step(
    nr, nz,
    query_feats, key_feats, value_feats, target, token_rates, row_reach, view_counts,
    w_first, w_third, w_second,
):
    _, row_count, cols, width = query_feats.shape
    tokens = row_count * cols
    hid = width // nr
    edge = HALO * cols
    heads = width // ATT_HD
    pieces = 3 * PER
    anywhere = pl.BlockSpec(memory_space=pl.ANY)
    flat = lambda a: a.reshape(tokens, width)
    out = pl.pallas_call(
        functools.partial(step_kernel, nr, nz, cols),
        out_shape=pltpu.VMEM((tokens, width), BF16),
        in_specs=[anywhere] * 5 + [pl.BlockSpec(memory_space=pltpu.HBM)] * 2 + [anywhere] * 3,
        out_specs=pl.BlockSpec(memory_space=pltpu.VMEM),
        scratch_shapes=[
            pltpu.VMEM((tokens, width), BF16),
            pltpu.VMEM((2, tokens, width), BF16),
            pltpu.VMEM((tokens, width), BF16),
            pltpu.VMEM((1, tokens), F32),
            pltpu.SMEM((row_count,), jnp.int32),
            pltpu.SMEM((1,), jnp.int32),
            pltpu.VMEM((width, 2 * hid), BF16),
            pltpu.VMEM((hid, width), BF16),
            pltpu.VMEM((2, 2 * edge, width), BF16),
            pltpu.VMEM((nr, heads, tokens, ATT_HD), BF16),
            pltpu.VMEM((nr, tokens, width), BF16),
            pltpu.VMEM((nr, tokens, 128), F32),
            pltpu.VMEM((4, 8, 128), F32),
            pltpu.VMEM((3 * hid, width), F32),
            pltpu.VMEM((3 * hid, width), BF16),
            pltpu.VMEM((3 * hid, width), BF16),
            pltpu.VMEM((3 * hid, width), BF16),
            pltpu.VMEM((3 * hid, width), F32),
            pltpu.VMEM((2 * hid, width), F32),
            pltpu.VMEM((nr, 4, width), F32),
            pltpu.VMEM((2 * hid, width), BF16),
            pltpu.VMEM((nr - 1, tokens, width), BF16),
            pltpu.VMEM((nr - 1, tokens, width), BF16),
            pltpu.SemaphoreType.DMA((10,)),
            pltpu.SemaphoreType.DMA((4 + nr,)),
            pltpu.SemaphoreType.DMA((9 + nr,)),
            pltpu.SemaphoreType.DMA((nr - 1, heads)),
            pltpu.SemaphoreType.DMA((4,)),
            pltpu.SemaphoreType.DMA((pieces,)),
            pltpu.SemaphoreType.DMA((pieces,)),
        ],
        compiler_params=pltpu.CompilerParams(collective_id=0, has_side_effects=True),
    )(
        flat(query_feats), flat(key_feats), flat(value_feats), flat(target),
        token_rates.reshape(1, tokens), row_reach, view_counts,
        w_first.reshape(width, width), w_third.reshape(width, width), w_second.reshape(width, width),
    )
    return out.reshape(query_feats.shape)


def solution(mesh):
    placed = (
        P("view", "row", None, "head"),
        P("view", "row", None, "head"),
        P("view", "row", None, "head"),
        P("view", "row", None, "head"),
        P("view", "head", "row"),
        P("row"),
        P("view"),
        P("head", None, None),
        P("head", None, None),
        P("head", None, None),
    )
    nr, nz = mesh.shape["row"], mesh.shape["view"]
    fits = nr == 4 and nz == 4 and HD % (128 * nr) == 0 and HD % (16 * nr * PER) == 0
    return jax.shard_map(
        functools.partial(fused_step, nr, nz) if fits else per_device,
        mesh=mesh,
        in_specs=placed,
        out_specs=P("view", "row", None, "head"),
        check_vma=False,
    )
```

time: 42.3 us -> 39.8 us (0.941)
  Pallas kernels: 40.5 us -> 38 us
    pallas_call x1, Pallas kernels: 40.5 us -> 38 us  [fused_step(): pl.pallas_call(functools.partial(step_kernel, nr, nz, cols), out_shape=pl...]
where the time goes in v1:
time: 39.8 us; the launch traced here: 39.3 us
  Pallas kernels  38 us (95%)
  local copies, waits for them, and re-layouts  0.66 us (2%)
  between operations  0.66 us (2%)
    pallas_call x1, Pallas kernels, fused_step(): pl.pallas_call(functools.partial(step_kernel, nr, nz, cols), out_shape=pl...  38 us

profile of v1, /device:TPU:1, one launch (start us, length us, event | category | flops | bytes accessed | tf_op | source)
XLA Modules:
  0.0 39.3 jit_solution(13390040427084001786)
XLA Ops:
  0.7 38.0 %shard_map.100 = bf16[128,512]{1,0:T(8,128)(2,1)S(1)} custom-call(bf16[128,512]{1,0:T(8,128)(2,1)} %bitcast.13, bf16[128,512]{1,0:T(8,128)(2,1)} %bitcast.14, bf16[128,512]{1,0:T(8,128)(2,1)} %bitcast.15, bf16[128,512]{1,0:T(8,128)(2,1)} %bitcast.16, f32[1,128]{1,0:T(1,128)} %bitcast.17, s32[8]{0:T(128)} %reach_hbm.1, s32[1]{0:T(128)S(6)} %copy.13.count_hbm, ...), custom_call_target="tpu_custom_call" | custom-call | tf_op jit(solution)/shard_map/pallas_call | solution.py:572
  38.6 0.7 %copy.12 = bf16[1,8,16,512]{3,2,1,0:T(8,128)(2,1)} copy(bf16[1,8,16,512]{3,2,1,0:T(8,128)(2,1)S(1)} %bitcast.9) | data formatting | bytes 262144

commit v2 on v1

--- a/solution.py
+++ b/solution.py
@@ -11,7 +11,10 @@
 HD = 512
 ATT_HD = 128
 HALO = 2
-PER = 4
+PER = 8
+LAGS = (9, 8)
+LEADS = (24, 24)
+HOLD = 20
 MESH = pl.DeviceIdType.MESH
 BF16 = jnp.bfloat16
 F32 = jnp.float32
@@ -187,8 +190,9 @@
     nr, nz, cols,
     q_hbm, k_hbm, v_hbm, t_hbm, rates_hbm, reach_hbm, count_hbm, wf_hbm, wt_hbm, ws_hbm,
     out_ref,
-    q_ref, kv_ref, t_ref, rates_ref, reach_ref, count_ref, wft, ws, halo, raw, sall, norms, cnt, gfull, gsum, gin, gtot,
-    wold, wnew, ss, mixed, osend, orecv, load_sem, row_send, row_recv, k_recv, view_send, out_recv, total_recv,
+    q_ref, kv_ref, t_ref, rates_ref, reach_ref, count_ref, wft, ws, halo, raw, sall, cnt, gout, gside, gfull, gsum, gin, gtot,
+    wold, news, ss,
+    load_sem, row_send, row_recv, k_recv, view_send, side_recv, out_recv, total_recv, near_recv, far_recv, on_recv,
 ):
     tokens, width = q_ref.shape
     rows_here = tokens // cols
@@ -200,7 +204,10 @@
     per = pieces // 3
     me = lax.axis_index("row")
     mz = lax.axis_index("view")
+    partner, across = flip(me, 1), flip(me, 2)
+    above, below = me + 1, me - 1
     mine = pl.ds(pl.multiple_of(me * hid, hid), hid)
+    theirs = pl.ds(pl.multiple_of(across * hid, hid), hid)
     low = mz < nz // 2
     inner = jnp.where(low, mz + 1, mz - 1)
     outer = jnp.where(low, mz - 1, mz + 1)
@@ -219,12 +226,13 @@
         pl.semaphore_signal(barrier, inc=1, device_id={"view": outer}, device_id_type=MESH)
 
     loads = [
-        pltpu.make_async_copy(source, target, load_sem.at[i])
+        pltpu.make_async_copy(source, target, load_sem.at[min(i, 7) if i < 11 else 8])
         for i, (source, target) in enumerate((
             (k_hbm, kv_ref.at[0]), (v_hbm, kv_ref.at[1]), (count_hbm, count_ref), (reach_hbm, reach_ref),
             (t_hbm, t_ref), (rates_hbm, rates_ref), (q_hbm, q_ref),
-            (wf_hbm.at[:, mine], wft.at[:, pl.ds(0, hid)]), (wt_hbm.at[:, mine], wft.at[:, pl.ds(hid, hid)]),
-            (ws_hbm.at[mine, :], ws),
+            (wf_hbm.at[:, theirs], wft.at[:, pl.ds(0, hid)]), (wt_hbm.at[:, theirs], wft.at[:, pl.ds(hid, hid)]),
+            (wf_hbm.at[:, mine], wft.at[:, pl.ds(2 * hid, hid)]), (wt_hbm.at[:, mine], wft.at[:, pl.ds(3 * hid, hid)]),
+            (ws_hbm.at[theirs, :], ws.at[pl.ds(0, hid)]), (ws_hbm.at[mine, :], ws.at[pl.ds(hid, hid)]),
         ))
     ]
     for load in loads:
@@ -236,9 +244,6 @@
             device_id={axis: peer}, device_id_type=MESH,
         )
 
-    partner, across = flip(me, 1), flip(me, 2)
-    above, below = me + 1, me - 1
-
     @pl.when(me == 0)
     def _():
         halo[:, :edge] = jnp.zeros((2, edge, width), BF16)
@@ -249,6 +254,26 @@
 
     row_base = me * rows_here
     tok_base = me * tokens
+
+    pl.semaphore_wait(barrier, nr + jnp.where(center, 1, 0))
+
+    @pl.when(has_above)
+    def _():
+        for i, source in enumerate((k_hbm, v_hbm)):
+            remote(
+                source.at[pl.ds(tokens - edge, edge)], halo.at[i, pl.ds(0, edge)], row_send.at[0], row_recv.at[0], "row", above
+            ).start()
+
+    @pl.when(has_below)
+    def _():
+        for i, source in enumerate((k_hbm, v_hbm)):
+            remote(
+                source.at[pl.ds(0, edge)], halo.at[i, pl.ds(edge, edge)], row_send.at[1], row_recv.at[1], "row", below
+            ).start()
+
+    up_halo = remote(halo.at[:, pl.ds(edge, edge)], halo.at[:, pl.ds(0, edge)], row_send.at[0], row_recv.at[0], "row", above)
+    down_halo = remote(halo.at[:, pl.ds(0, edge)], halo.at[:, pl.ds(edge, edge)], row_send.at[1], row_recv.at[1], "row", below)
+
     for load in loads[2:4]:
         load.wait()
     view_total = count_ref[0]
@@ -261,30 +286,11 @@
         load.wait()
     rate_col = jnp.sum(jnp.where(sub == lane, rates_ref[...], 0.0), axis=1, keepdims=True)
     sall[0] = (rate_col * valid_col * t_ref[...].astype(F32)).astype(BF16)
-    for load in loads[:2]:
-        load.wait()
-
-    pl.semaphore_wait(barrier, nr + jnp.where(center, 1, 0))
-
-    up_halo = remote(kv_ref.at[:, pl.ds(tokens - edge, edge)], halo.at[:, pl.ds(0, edge)], row_send.at[0], row_recv.at[0], "row", above)
-    down_halo = remote(kv_ref.at[:, pl.ds(0, edge)], halo.at[:, pl.ds(edge, edge)], row_send.at[1], row_recv.at[1], "row", below)
-
-    @pl.when(has_above)
-    def _():
-        up_halo.start()
-
-    @pl.when(has_below)
-    def _():
-        down_halo.start()
-
     s_near = remote(sall.at[0], sall.at[1], row_send.at[2], row_recv.at[2], "row", partner)
-    s_far = remote(sall.at[0], sall.at[2], row_send.at[2], row_recv.at[3], "row", across)
-    s_on = remote(sall.at[2], sall.at[3], row_send.at[2], row_recv.at[4], "row", partner)
     s_near.start()
-    s_far.start()
-    cnt_up = remote(cnt.at[0], cnt.at[1], view_send.at[0], row_recv.at[8], "view", inner)
-    cnt_mid = remote(cnt.at[2], cnt.at[3], view_send.at[0], row_recv.at[9], "view", inner)
-    cnt_down = remote(cnt.at[3], cnt.at[3], view_send.at[1], row_recv.at[9], "view", outer)
+    cnt_up = remote(cnt.at[0], cnt.at[1], view_send.at[0], row_recv.at[3], "view", inner)
+    cnt_mid = remote(cnt.at[2], cnt.at[3], view_send.at[0], row_recv.at[4], "view", inner)
+    cnt_down = remote(cnt.at[3], cnt.at[3], view_send.at[1], row_recv.at[4], "view", outer)
 
     @pl.when(leaf)
     def _():
@@ -305,23 +311,41 @@
         )
 
     near_ok = allowed(sub, lane)
-    far_q = lax.broadcasted_iota(jnp.int32, (tokens, 2 * edge), 0)
-    far_k = lax.broadcasted_iota(jnp.int32, (tokens, 2 * edge), 1)
-    far_ok = allowed(far_q, jnp.where(far_k < edge, far_k - edge, far_k - edge + tokens))
+    far_q = lax.broadcasted_iota(jnp.int32, (2 * edge, 2 * edge), 0)
+    far_k = lax.broadcasted_iota(jnp.int32, (2 * edge, 2 * edge), 1)
+    far_ok = allowed(
+        jnp.where(far_q < edge, far_q, far_q - 2 * edge + tokens),
+        jnp.where(far_k < edge, far_k - edge, far_k - edge + tokens),
+    )
     root = 1.0 / math.sqrt(ATT_HD)
     spans = [slice(h * ATT_HD, (h + 1) * ATT_HD) for h in range(heads)]
-    loads[6].wait()
+    for load in loads[:2] + loads[6:7]:
+        load.wait()
+    inside = slice(edge, tokens - edge)
+    ends = (slice(0, edge), slice(tokens - edge, tokens))
+
+    def outer_rows(value):
+        return jnp.concatenate([value[e] for e in ends], axis=0)
+
+    def pass_keys(at, receives):
+        return remote(raw.at[0, :, at], raw.at[1, :, at], row_send.at[3], receives, "row", partner)
+
     near = []
-    for hs in spans:
+    for h, hs in enumerate(spans):
         scores = jnp.where(near_ok, dot(q_ref[:, hs], kv_ref[0, :, hs], NT) * root, -1e30)
         top = jnp.max(scores, axis=-1, keepdims=True)
         power = jnp.exp(scores - top)
-        near.append((top, jnp.sum(power, axis=-1, keepdims=True), dot(power.astype(BF16), kv_ref[1, :, hs])))
-    for load in loads[7:]:
-        load.wait()
-    wold[0:hid] = wft[:, :hid].astype(F32).T
-    wold[hid:2 * hid] = wft[:, hid:].astype(F32).T
-    wold[2 * hid:] = ws[...].astype(F32)
+        total = jnp.sum(power, axis=-1, keepdims=True)
+        mix = dot(power.astype(BF16), kv_ref[1, :, hs])
+        raw[0, h, inside] = (mix[inside] * (1.0 / total[inside])).astype(BF16)
+        near.append((outer_rows(top), outer_rows(total), outer_rows(mix), outer_rows(q_ref.at[:, hs])))
+    middle = pass_keys(pl.ds(edge, tokens - 2 * edge), k_recv.at[0])
+    middle.start()
+    pltpu.make_async_copy(wft, wft, load_sem.at[7]).wait()
+    pltpu.make_async_copy(ws, ws, load_sem.at[8]).wait()
+    wold[0:hid] = wft[:, 2 * hid:3 * hid].astype(F32).T
+    wold[hid:2 * hid] = wft[:, 3 * hid:].astype(F32).T
+    wold[2 * hid:] = ws[hid:].astype(F32)
 
     @pl.when(has_below)
     def _():
@@ -331,32 +355,33 @@
     def _():
         down_halo.wait_recv()
 
-    k_near, k_far, k_on = [], [], []
     for h, hs in enumerate(spans):
-        near_top, near_sum, near_out = near[h]
-        far = jnp.where(far_ok, dot(q_ref[:, hs], halo[0, :, hs], NT) * root, -1e30)
+        near_top, near_sum, near_out, queries = near[h]
+        far = jnp.where(far_ok, dot(queries, halo[0, :, hs], NT) * root, -1e30)
         top = jnp.maximum(near_top, jnp.max(far, axis=-1, keepdims=True))
         power = jnp.exp(far - top)
         keep = jnp.exp(near_top - top)
         inverse = 1.0 / (keep * near_sum + jnp.sum(power, axis=-1, keepdims=True))
         mix = keep * near_out + dot(power.astype(BF16), halo[1, :, hs])
-        raw[0, h] = (mix * inverse).astype(BF16)
-        k_near.append(remote(raw.at[0, h], raw.at[1, h], row_send.at[3], k_recv.at[0, h], "row", partner))
-        k_far.append(remote(raw.at[0, h], raw.at[2, h], row_send.at[3], k_recv.at[1, h], "row", across))
-        k_on.append(remote(raw.at[2, h], raw.at[3, h], row_send.at[3], k_recv.at[2, h], "row", partner))
-        k_far[h].start()
-        k_near[h].start()
-
-    def block(d):
-        keys = jnp.concatenate([raw[d, h] for h in range(heads)], axis=1)
-        both = dot(keys, wft[...])
-        back = dot(sall[d], ws[...], NT)
+        mix = (mix * inverse).astype(BF16)
+        raw[0, h, ends[0]] = mix[:edge]
+        raw[0, h, ends[1]] = mix[edge:]
+    for e in ends:
+        pass_keys(pl.ds(e.start, edge), k_recv.at[1]).start()
+
+    def token_norm(d):
         total_sq = jnp.zeros((tokens, ATT_HD), F32)
         for h in range(heads):
             part = raw[d, h].astype(F32)
             total_sq = total_sq + part * part
-        norm = lax.rsqrt(jnp.sum(total_sq, axis=-1, keepdims=True) * (1.0 / width) + 1e-06)
-        norms[d] = jnp.broadcast_to(norm, (tokens, 128))
+        return lax.rsqrt(jnp.sum(total_sq, axis=-1, keepdims=True) * (1.0 / width) + 1e-06)
+
+    def keys_of(d):
+        return jnp.concatenate([raw[d, h] for h in range(heads)], axis=1)
+
+    def block(d, keys, norm, half):
+        both = dot(keys, wft[:, half * 2 * hid:(half + 1) * 2 * hid])
+        back = dot(sall[d], ws[half * hid:(half + 1) * hid], NT)
         first = both[:, :hid] * norm
         third = both[:, hid:] * norm
         sig = jax.nn.sigmoid(first)
@@ -369,20 +394,17 @@
             ],
             axis=1,
         )
-        return left, keys, (gate * third).astype(BF16)
-
-    def grads(d, first_block):
-        left, keys, gated = block(d)
-        grad = dot(left, keys, TN)
-        gfull[: 2 * hid] = grad if first_block else gfull[: 2 * hid] + grad
-        grad = dot(gated, sall[d], TN)
-        gfull[2 * hid:] = grad if first_block else gfull[2 * hid:] + grad
-
-    grads(0, True)
-    s_near.wait_recv()
-    for copy in k_near:
-        copy.wait_recv()
-    grads(1, False)
+        return left, (gate * third).astype(BF16)
+
+    def rows(i):
+        return pl.ds(i * piece, piece)
+
+    def aside(i):
+        return remote(gout.at[rows(i)], gside.at[rows(i)], row_send.at[4], side_recv.at[i], "row", across)
+
+    own_keys = keys_of(0)
+    own_norm = token_norm(0)
+    own_blocks = [block(0, own_keys, own_norm, half) for half in range(2)]
 
     @pl.when(center)
     def _():
@@ -390,61 +412,59 @@
         cnt[2] = cnt[0] + cnt[1]
         cnt_mid.start()
 
-    s_far.wait_recv()
-    s_on.start()
-    for h in range(heads):
-        k_far[h].wait_recv()
-        k_on[h].start()
-    grads(2, False)
+    s_near.wait_recv()
+    middle.wait_recv()
+    pass_keys(pl.ds(0, 2 * edge), k_recv.at[1]).wait_recv()
+    next_keys = keys_of(1)
+    next_norm = token_norm(1)
+    keys = jnp.concatenate([own_keys, next_keys], axis=0)
+    steps = jnp.concatenate([sall[0], sall[1]], axis=0)
+    for half in range(2):
+        left, gated = (
+            jnp.concatenate(pair, axis=0) for pair in zip(own_blocks[half], block(1, next_keys, next_norm, half))
+        )
+        grad = dot(left, keys, TN)
+        if half == 0:
+            gout[: 2 * hid] = grad.astype(BF16)
+            for i in range(2 * per):
+                aside(i).start()
+        else:
+            gfull[: 2 * hid] = grad
+        grad = dot(gated, steps, TN)
+        if half == 0:
+            gout[2 * hid:] = grad.astype(BF16)
+            for i in range(2 * per, 3 * per):
+                aside(i).start()
+        else:
+            gfull[2 * hid:] = grad
 
     @pl.when(center)
     def _():
         cnt_mid.wait_recv()
         cnt[3] = cnt[2] + cnt[3]
         cnt_down.start()
-
-    s_on.wait_recv()
-    for copy in k_on:
-        copy.wait_recv()
-
-    def rows(i):
-        return pl.ds(i * piece, piece)
-
-    def rise(i, target, receives):
-        return remote(gsum.at[rows(i)], target.at[rows(i)], view_send.at[2], receives.at[i], "view", inner)
-
-    def fall(i):
-        return remote(gtot.at[rows(i)], gtot.at[rows(i)], view_send.at[3], total_recv.at[i], "view", outer)
-
-    left, keys, gated = block(3)
-    grad = gfull[: 2 * hid] + dot(left, keys, TN)
-    gfull[: 2 * hid] = grad
-
-    @pl.when(leaf)
-    def _():
-        for i in range(2 * per):
-            gsum[rows(i)] = gfull[rows(i)].astype(BF16)
-            rise(i, gin, out_recv).start()
-
-    grad = gfull[2 * hid:] + dot(gated, sall[3], TN)
-    gfull[2 * hid:] = grad
-
-    @pl.when(leaf)
-    def _():
-        for i in range(2 * per, 3 * per):
-            gsum[rows(i)] = gfull[rows(i)].astype(BF16)
-            rise(i, gin, out_recv).start()
-        cnt_down.wait_recv()
 
     ss[0, 2:3] = jnp.sum(wold[:hid] * wold[:hid], axis=0, keepdims=True)
     ss[0, 3:4] = jnp.sum(wold[hid:2 * hid] * wold[hid:2 * hid], axis=0, keepdims=True)
     second_old = wold[2 * hid:]
     second_size = jnp.sqrt(jnp.sum(second_old * second_old, axis=-1, keepdims=True) + 1e-06)
-    share_total = 1.0 / cnt[3, 0:1, 0:1]
+
+    def rise(i, target, receives):
+        return remote(gsum.at[rows(i)], target.at[rows(i)], view_send.at[2], receives.at[i], "view", inner)
+
+    def fall(i):
+        return remote(gtot.at[rows(i)], gtot.at[rows(i)], view_send.at[3], total_recv.at[i], "view", outer)
+
+    def lift(i):
+        aside(i).wait_recv()
+        gsum[rows(i)] = (gfull[rows(i)] + gside[rows(i)].astype(F32)).astype(BF16)
+        rise(i, gin, out_recv).start()
 
     def join(i):
+        aside(i).wait_recv()
+        partial = gfull[rows(i)] + gside[rows(i)].astype(F32)
         rise(i, gin, out_recv).wait_recv()
-        gsum[rows(i)] = (gfull[rows(i)] + gin[rows(i)].astype(F32)).astype(BF16)
+        gsum[rows(i)] = (partial + gin[rows(i)].astype(F32)).astype(BF16)
         rise(i, gtot, total_recv).start()
 
     def finish(i):
@@ -452,43 +472,71 @@
         gtot[rows(i)] = (gsum[rows(i)].astype(F32) + gtot[rows(i)].astype(F32)).astype(BF16)
         fall(i).start()
 
-    lag = 3
-
-    @pl.when(center)
-    def _():
-        for i in range(lag):
-            join(i)
+    roles = (
+        (low & center, join, finish, LAGS[0]),
+        (~low & center, join, finish, LAGS[1]),
+        (low & leaf, lift, None, LEADS[0]),
+        (~low & leaf, lift, None, LEADS[1]),
+    )
+    for role, begin, _, ahead in roles:
+        @pl.when(role)
+        def _():
+            for i in range(ahead):
+                begin(i)
+            if begin is lift:
+                cnt_down.wait_recv()
+
+    share_total = 1.0 / cnt[3, 0:1, 0:1]
 
     def arrive(i):
-        @pl.when(center)
-        def _():
-            if i + lag < pieces:
-                join(i + lag)
-            finish(i)
-
-    def land(i):
-        @pl.when(leaf)
-        def _():
-            fall(i).wait_recv()
+        for role, begin, end, ahead in roles:
+            @pl.when(role)
+            def _():
+                if i + ahead < pieces:
+                    begin(i + ahead)
+                if end is None:
+                    fall(i).wait_recv()
+                else:
+                    end(i)
 
     def raise_rows(i):
         raised = wold[rows(i)] + gtot[rows(i)].astype(F32) * share_total
         if i < 2 * per:
-            wnew[rows(i)] = raised
+            news[0, rows(i)] = raised.astype(BF16)
             return jnp.sum(raised * raised, axis=0, keepdims=True)
         at = (i - 2 * per) * piece
         size = jnp.sqrt(jnp.sum(raised * raised, axis=-1, keepdims=True) + 1e-06)
-        ws[at:at + piece] = (raised * (second_size[at:at + piece] / size)).astype(BF16)
+        news[0, rows(i)] = (raised * (second_size[at:at + piece] / size)).astype(BF16)
+
+    groups = [(0, per), (per, 2 * per), (2 * per, 3 * per - 2), (3 * per - 2, 3 * per - 1), (3 * per - 1, 3 * per)]
+
+    def span(group):
+        return pl.ds(group[0] * piece, (group[1] - group[0]) * piece)
+
+    def lend(i):
+        return remote(news.at[0, rows(i)], news.at[2, rows(i)], row_send.at[5], far_recv.at[i], "row", across)
+
+    def pair(g, slot, receives):
+        return remote(
+            news.at[slot, span(groups[g])], news.at[slot + 1, span(groups[g])], row_send.at[5], receives.at[g], "row", partner
+        )
+
+    def relay(i):
+        lend(i).wait_recv()
+        for g, group in enumerate(groups):
+            if group[1] == i + 1:
+                pair(g, 2, on_recv).start()
 
     ss_copies = [
-        remote(ss.at[0], ss.at[d], row_send.at[3 + d], row_recv.at[4 + d], "row", flip(me, d)) for d in range(1, nr)
+        remote(ss.at[0], ss.at[d], row_send.at[5 + d], row_recv.at[4 + d], "row", flip(me, d)) for d in range(1, nr)
     ]
     for i in range(pieces):
         arrive(i)
-        if i == pieces - 1:
-            break
-        land(i)
         square = raise_rows(i)
+        lend(i).start()
+        for g, group in enumerate(groups):
+            if group[1] == i + 1:
+                pair(g, 0, near_recv).start()
         if i < 2 * per:
             running = square if i % per == 0 else running + square
             if i % per == per - 1:
@@ -497,41 +545,44 @@
                 if m == 1:
                     for copy in ss_copies:
                         copy.start()
+        if i >= HOLD:
+            relay(i - HOLD)
+    for i in range(pieces - HOLD, 2 * per):
+        relay(i)
     for copy in ss_copies:
         copy.wait_recv()
     sums = ss[0]
     for d in range(1, nr):
         sums = sums + ss[d]
     scales = jnp.sqrt(sums[2:4] + 1e-06) / jnp.sqrt(sums[0:2] + 1e-06)
-    mixed[:hid] = (wnew[:hid] * scales[0:1]).astype(BF16)
-    mixed[hid:] = (wnew[hid:] * scales[1:2]).astype(BF16)
-    order = list(range(3, nr, 2)) + list(range(2, nr, 2)) + [1, 0]
-    applied = {}
-    for d in order:
-        keys = jnp.concatenate([raw[d, h] for h in range(heads)], axis=1)
-        both = dot(keys, mixed[...], NT)
-        first = both[:, :hid] * norms[d][:, 0:1]
-        third = both[:, hid:] * norms[d][:, 0:1]
-        applied[d] = (first * jax.nn.sigmoid(first) * third).astype(BF16)
-    land(pieces - 1)
-    raise_rows(pieces - 1)
-
-    def leave(d, peer):
-        return remote(osend.at[d - 1], orecv.at[d - 1], row_send.at[nr + 3], row_recv.at[9 + d], "row", peer)
-
-    o_copies = {1: leave(1, partner), 2: leave(2, across), 3: leave(3, partner)}
-    for d in order:
-        total = dot(applied[d], ws[...])
-        if d == 0:
-            continue
-        if d % 2 == 0:
-            o_copies[d + 1].wait_recv()
-            total = total + orecv[d].astype(F32)
-        osend[d - 1] = total.astype(BF16)
-        o_copies[d].start()
-    for d in [1] + list(range(2, nr, 2)):
-        o_copies[d].wait_recv()
-        total = total + orecv[d - 1].astype(F32)
+    wide = own_keys.astype(F32)
+    scaled = [(wide * scales[m:m + 1]).astype(BF16) for m in range(2)]
+
+    def apply(slot):
+        first = dot(scaled[0], news[slot, :hid], NT) * own_norm
+        third = dot(scaled[1], news[slot, hid:2 * hid], NT) * own_norm
+        return (first * jax.nn.sigmoid(first) * third).astype(BF16)
+
+    applied = [apply(0)]
+    for g in range(2):
+        pair(g, 0, near_recv).wait_recv()
+    applied.append(apply(1))
+    applied.append(apply(2))
+    for i in range(max(pieces - HOLD, 2 * per), groups[2][1]):
+        relay(i)
+    for g in range(2):
+        pair(g, 2, on_recv).wait_recv()
+    applied.append(apply(3))
+    for i in range(max(pieces - HOLD, groups[2][1]), pieces):
+        relay(i)
+    total = dot(applied[0], news[0, 2 * hid:])
+    for g in range(2, len(groups)):
+        pair(g, 0, near_recv).wait_recv()
+    total = total + dot(applied[1], news[1, 2 * hid:])
+    total = total + dot(applied[2], news[2, 2 * hid:])
+    for g in range(2, len(groups)):
+        pair(g, 2, on_recv).wait_recv()
+    total = total + dot(applied[3], news[3, 2 * hid:])
     out_ref[...] = total.astype(BF16)
 
     @pl.when(has_above)
@@ -542,9 +593,10 @@
     def _():
         down_halo.wait_send()
 
-    remote(sall.at[pl.ds(0, nr - 1)], sall.at[pl.ds(0, nr - 1)], row_send.at[2], row_recv.at[2], "row", partner).wait_send()
-    remote(raw.at[pl.ds(0, nr - 1)], raw.at[pl.ds(0, nr - 1)], row_send.at[3], row_recv.at[2], "row", partner).wait_send()
-    remote(osend, orecv, row_send.at[nr + 3], row_recv.at[2], "row", partner).wait_send()
+    s_near.wait_send()
+    remote(raw.at[0], raw.at[1], row_send.at[3], row_recv.at[2], "row", partner).wait_send()
+    remote(gout, gside, row_send.at[4], row_recv.at[2], "row", across).wait_send()
+    remote(news.at[pl.ds(0, 3)], news.at[pl.ds(0, 3)], row_send.at[5], row_recv.at[2], "row", partner).wait_send()
     for copy in ss_copies:
         copy.wait_send()
     remote(gsum, gin, view_send.at[2], row_recv.at[2], "view", inner).wait_send()
@@ -581,30 +633,32 @@
             pltpu.VMEM((1, tokens), F32),
             pltpu.SMEM((row_count,), jnp.int32),
             pltpu.SMEM((1,), jnp.int32),
-            pltpu.VMEM((width, 2 * hid), BF16),
-            pltpu.VMEM((hid, width), BF16),
+            pltpu.VMEM((width, 4 * hid), BF16),
+            pltpu.VMEM((2 * hid, width), BF16),
             pltpu.VMEM((2, 2 * edge, width), BF16),
-            pltpu.VMEM((nr, heads, tokens, ATT_HD), BF16),
-            pltpu.VMEM((nr, tokens, width), BF16),
-            pltpu.VMEM((nr, tokens, 128), F32),
+            pltpu.VMEM((2, heads, tokens, ATT_HD), BF16),
+            pltpu.VMEM((2, tokens, width), BF16),
             pltpu.VMEM((4, 8, 128), F32),
+            pltpu.VMEM((3 * hid, width), BF16),
+            pltpu.VMEM((3 * hid, width), BF16),
             pltpu.VMEM((3 * hid, width), F32),
             pltpu.VMEM((3 * hid, width), BF16),
             pltpu.VMEM((3 * hid, width), BF16),
             pltpu.VMEM((3 * hid, width), BF16),
             pltpu.VMEM((3 * hid, width), F32),
-            pltpu.VMEM((2 * hid, width), F32),
+            pltpu.VMEM((nr, 3 * hid, width), BF16),
             pltpu.VMEM((nr, 4, width), F32),
-            pltpu.VMEM((2 * hid, width), BF16),
-            pltpu.VMEM((nr - 1, tokens, width), BF16),
-            pltpu.VMEM((nr - 1, tokens, width), BF16),
-            pltpu.SemaphoreType.DMA((10,)),
+            pltpu.SemaphoreType.DMA((9,)),
+            pltpu.SemaphoreType.DMA((5 + nr,)),
             pltpu.SemaphoreType.DMA((4 + nr,)),
-            pltpu.SemaphoreType.DMA((9 + nr,)),
-            pltpu.SemaphoreType.DMA((nr - 1, heads)),
+            pltpu.SemaphoreType.DMA((2,)),
             pltpu.SemaphoreType.DMA((4,)),
             pltpu.SemaphoreType.DMA((pieces,)),
             pltpu.SemaphoreType.DMA((pieces,)),
+            pltpu.SemaphoreType.DMA((pieces,)),
+            pltpu.SemaphoreType.DMA((5,)),
+            pltpu.SemaphoreType.DMA((pieces,)),
+            pltpu.SemaphoreType.DMA((5,)),
         ],
         compiler_params=pltpu.CompilerParams(collective_id=0, has_side_effects=True),
     )(

time: 39.8 us -> 34.5 us (0.87)
  Pallas kernels: 38 us -> 33.1 us
    pallas_call x1, Pallas kernels: 38 us -> 33.1 us  [fused_step(): pl.pallas_call(functools.partial(step_kernel, nr, nz, cols), out_shape=pl...]
where the time goes in v2:
time: 34.5 us; the launch traced here: 34.4 us
  Pallas kernels  33.1 us (96%)
  local copies, waits for them, and re-layouts  0.66 us (2%)
  between operations  0.66 us (2%)
    pallas_call x1, Pallas kernels, fused_step(): pl.pallas_call(functools.partial(step_kernel, nr, nz, cols), out_shape=pl...  33.1 us

profile of v2, /device:TPU:1, one launch (start us, length us, event | category | flops | bytes accessed | tf_op | source)
XLA Modules:
  0.0 34.4 jit_solution(12271808950367750394)
XLA Ops:
  0.7 33.1 %shard_map.100 = bf16[128,512]{1,0:T(8,128)(2,1)S(1)} custom-call(bf16[128,512]{1,0:T(8,128)(2,1)} %bitcast.13, bf16[128,512]{1,0:T(8,128)(2,1)} %bitcast.14, bf16[128,512]{1,0:T(8,128)(2,1)} %bitcast.15, bf16[128,512]{1,0:T(8,128)(2,1)} %bitcast.16, f32[1,128]{1,0:T(1,128)} %bitcast.17, s32[8]{0:T(128)} %reach_hbm.1, s32[1]{0:T(128)S(6)} %copy.13.count_hbm, ...), custom_call_target="tpu_custom_call" | custom-call | tf_op jit(solution)/shard_map/pallas_call | solution.py:624
  33.7 0.7 %copy.12 = bf16[1,8,16,512]{3,2,1,0:T(8,128)(2,1)} copy(bf16[1,8,16,512]{3,2,1,0:T(8,128)(2,1)S(1)} %bitcast.9) | data formatting | bytes 262144

commit v3 on v2

--- a/solution.py
+++ b/solution.py
@@ -12,9 +12,9 @@
 ATT_HD = 128
 HALO = 2
 PER = 8
-LAGS = (9, 8)
+SKIP = 4
+LAGS = (9, 9)
 LEADS = (24, 24)
-HOLD = 20
 MESH = pl.DeviceIdType.MESH
 BF16 = jnp.bfloat16
 F32 = jnp.float32
@@ -190,9 +190,9 @@
     nr, nz, cols,
     q_hbm, k_hbm, v_hbm, t_hbm, rates_hbm, reach_hbm, count_hbm, wf_hbm, wt_hbm, ws_hbm,
     out_ref,
-    q_ref, kv_ref, t_ref, rates_ref, reach_ref, count_ref, wft, ws, halo, raw, sall, cnt, gout, gside, gfull, gsum, gin, gtot,
+    q_ref, kv_ref, t_ref, rates_ref, reach_ref, count_ref, wft, ws, halo, raw, sall, cnt, gout, gside, gslant, gfull, gsum, gin, gtot,
     wold, news, ss,
-    load_sem, row_send, row_recv, k_recv, view_send, side_recv, out_recv, total_recv, near_recv, far_recv, on_recv,
+    load_sem, row_send, row_recv, halo_recv, k_recv, view_send, side_recv, total_recv, near_recv, far_recv, on_recv,
 ):
     tokens, width = q_ref.shape
     rows_here = tokens // cols
@@ -221,6 +221,9 @@
         pl.semaphore_signal(barrier, inc=1, device_id={"row": flip(me, d)}, device_id_type=MESH)
     pl.semaphore_signal(barrier, inc=1, device_id={"view": inner}, device_id_type=MESH)
 
+    slant = jnp.where(center, outer, inner)
+    pl.semaphore_signal(barrier, inc=1, device_id={"row": across, "view": slant}, device_id_type=MESH)
+
     @pl.when(center)
     def _():
         pl.semaphore_signal(barrier, inc=1, device_id={"view": outer}, device_id_type=MESH)
@@ -255,20 +258,20 @@
     row_base = me * rows_here
     tok_base = me * tokens
 
-    pl.semaphore_wait(barrier, nr + jnp.where(center, 1, 0))
+    pl.semaphore_wait(barrier, nr + 1 + jnp.where(center, 1, 0))
 
     @pl.when(has_above)
     def _():
         for i, source in enumerate((k_hbm, v_hbm)):
             remote(
-                source.at[pl.ds(tokens - edge, edge)], halo.at[i, pl.ds(0, edge)], row_send.at[0], row_recv.at[0], "row", above
+                source.at[pl.ds(tokens - edge, edge)], halo.at[i, pl.ds(0, edge)], row_send.at[0], halo_recv.at[0, i], "row", above
             ).start()
 
     @pl.when(has_below)
     def _():
         for i, source in enumerate((k_hbm, v_hbm)):
             remote(
-                source.at[pl.ds(0, edge)], halo.at[i, pl.ds(edge, edge)], row_send.at[1], row_recv.at[1], "row", below
+                source.at[pl.ds(0, edge)], halo.at[i, pl.ds(edge, edge)], row_send.at[1], halo_recv.at[1, i], "row", below
             ).start()
 
     up_halo = remote(halo.at[:, pl.ds(edge, edge)], halo.at[:, pl.ds(0, edge)], row_send.at[0], row_recv.at[0], "row", above)
@@ -286,11 +289,11 @@
         load.wait()
     rate_col = jnp.sum(jnp.where(sub == lane, rates_ref[...], 0.0), axis=1, keepdims=True)
     sall[0] = (rate_col * valid_col * t_ref[...].astype(F32)).astype(BF16)
-    s_near = remote(sall.at[0], sall.at[1], row_send.at[2], row_recv.at[2], "row", partner)
+    s_near = remote(sall.at[0], sall.at[1], row_send.at[2], row_recv.at[0], "row", partner)
     s_near.start()
-    cnt_up = remote(cnt.at[0], cnt.at[1], view_send.at[0], row_recv.at[3], "view", inner)
-    cnt_mid = remote(cnt.at[2], cnt.at[3], view_send.at[0], row_recv.at[4], "view", inner)
-    cnt_down = remote(cnt.at[3], cnt.at[3], view_send.at[1], row_recv.at[4], "view", outer)
+    cnt_up = remote(cnt.at[0], cnt.at[1], view_send.at[0], row_recv.at[1], "view", inner)
+    cnt_mid = remote(cnt.at[2], cnt.at[3], view_send.at[0], row_recv.at[2], "view", inner)
+    cnt_down = remote(cnt.at[3], cnt.at[3], view_send.at[1], row_recv.at[2], "view", outer)
 
     @pl.when(leaf)
     def _():
@@ -343,45 +346,30 @@
     middle.start()
     pltpu.make_async_copy(wft, wft, load_sem.at[7]).wait()
     pltpu.make_async_copy(ws, ws, load_sem.at[8]).wait()
-    wold[0:hid] = wft[:, 2 * hid:3 * hid].astype(F32).T
-    wold[hid:2 * hid] = wft[:, 3 * hid:].astype(F32).T
-    wold[2 * hid:] = ws[hid:].astype(F32)
-
-    @pl.when(has_below)
-    def _():
-        up_halo.wait_recv()
-
-    @pl.when(has_above)
-    def _():
-        down_halo.wait_recv()
-
-    for h, hs in enumerate(spans):
-        near_top, near_sum, near_out, queries = near[h]
-        far = jnp.where(far_ok, dot(queries, halo[0, :, hs], NT) * root, -1e30)
-        top = jnp.maximum(near_top, jnp.max(far, axis=-1, keepdims=True))
-        power = jnp.exp(far - top)
-        keep = jnp.exp(near_top - top)
-        inverse = 1.0 / (keep * near_sum + jnp.sum(power, axis=-1, keepdims=True))
-        mix = keep * near_out + dot(power.astype(BF16), halo[1, :, hs])
-        mix = (mix * inverse).astype(BF16)
-        raw[0, h, ends[0]] = mix[:edge]
-        raw[0, h, ends[1]] = mix[edge:]
-    for e in ends:
-        pass_keys(pl.ds(e.start, edge), k_recv.at[1]).start()
-
-    def token_norm(d):
-        total_sq = jnp.zeros((tokens, ATT_HD), F32)
-        for h in range(heads):
-            part = raw[d, h].astype(F32)
+    def halo_here(i):
+        @pl.when(has_below)
+        def _():
+            remote(halo.at[i, pl.ds(edge, edge)], halo.at[i, pl.ds(0, edge)], row_send.at[0], halo_recv.at[0, i], "row", above).wait_recv()
+
+        @pl.when(has_above)
+        def _():
+            remote(halo.at[i, pl.ds(0, edge)], halo.at[i, pl.ds(edge, edge)], row_send.at[1], halo_recv.at[1, i], "row", below).wait_recv()
+
+    def keys_of(d, rows_at):
+        return jnp.concatenate(
+            [jnp.concatenate([raw[d, h, at] for h in range(heads)], axis=1) for at in rows_at], axis=0
+        )
+
+    def token_norm(keys):
+        total_sq = jnp.zeros((keys.shape[0], ATT_HD), F32)
+        for hs in spans:
+            part = keys[:, hs].astype(F32)
             total_sq = total_sq + part * part
         return lax.rsqrt(jnp.sum(total_sq, axis=-1, keepdims=True) * (1.0 / width) + 1e-06)
 
-    def keys_of(d):
-        return jnp.concatenate([raw[d, h] for h in range(heads)], axis=1)
-
-    def block(d, keys, norm, half):
+    def block(keys, steps, norm, half):
         both = dot(keys, wft[:, half * 2 * hid:(half + 1) * 2 * hid])
-        back = dot(sall[d], ws[half * hid:(half + 1) * hid], NT)
+        back = dot(steps, ws[half * hid:(half + 1) * hid], NT)
         first = both[:, :hid] * norm
         third = both[:, hid:] * norm
         sig = jax.nn.sigmoid(first)
@@ -396,15 +384,48 @@
         )
         return left, (gate * third).astype(BF16)
 
+    def token_set(rows_at):
+        keys = jnp.concatenate([keys_of(d, rows_at) for d in range(2)], axis=0)
+        steps = jnp.concatenate([sall[d, at] for d in range(2) for at in rows_at], axis=0)
+        return keys, steps, token_norm(keys)
+
+    s_near.wait_recv()
+    middle.wait_recv()
+    inner_set = token_set((inside,))
+    inner_blocks = [block(*inner_set, half) for half in range(2)]
+    halo_here(0)
+    partly = []
+    for h, hs in enumerate(spans):
+        near_top, near_sum, near_out, queries = near[h]
+        far = jnp.where(far_ok, dot(queries, halo[0, :, hs], NT) * root, -1e30)
+        top = jnp.maximum(near_top, jnp.max(far, axis=-1, keepdims=True))
+        power = jnp.exp(far - top)
+        keep = jnp.exp(near_top - top)
+        inverse = 1.0 / (keep * near_sum + jnp.sum(power, axis=-1, keepdims=True))
+        partly.append((power.astype(BF16), keep * near_out, inverse))
+    halo_here(1)
+    for h, hs in enumerate(spans):
+        power, kept, inverse = partly[h]
+        mix = ((kept + dot(power, halo[1, :, hs])) * inverse).astype(BF16)
+        raw[0, h, ends[0]] = mix[:edge]
+        raw[0, h, ends[1]] = mix[edge:]
+    for e in ends:
+        pass_keys(pl.ds(e.start, edge), k_recv.at[1]).start()
+
     def rows(i):
         return pl.ds(i * piece, piece)
 
+    def skew(i):
+        return pltpu.make_async_remote_copy(
+            src_ref=gout.at[rows(i)], dst_ref=gslant.at[rows(i)], send_sem=row_send.at[4], recv_sem=side_recv.at[i],
+            device_id={"row": across, "view": inner}, device_id_type=MESH,
+        )
+
+    def early(i):
+        return remote(gsum.at[rows(i)], gin.at[rows(i)], view_send.at[2], side_recv.at[i], "view", inner)
+
     def aside(i):
         return remote(gout.at[rows(i)], gside.at[rows(i)], row_send.at[4], side_recv.at[i], "row", across)
-
-    own_keys = keys_of(0)
-    own_norm = token_norm(0)
-    own_blocks = [block(0, own_keys, own_norm, half) for half in range(2)]
 
     @pl.when(center)
     def _():
@@ -412,24 +433,38 @@
         cnt[2] = cnt[0] + cnt[1]
         cnt_mid.start()
 
-    s_near.wait_recv()
-    middle.wait_recv()
     pass_keys(pl.ds(0, 2 * edge), k_recv.at[1]).wait_recv()
-    next_keys = keys_of(1)
-    next_norm = token_norm(1)
-    keys = jnp.concatenate([own_keys, next_keys], axis=0)
-    steps = jnp.concatenate([sall[0], sall[1]], axis=0)
+    outer_set = token_set(ends)
+    keys, steps = (jnp.concatenate(pair, axis=0) for pair in zip(inner_set[:2], outer_set[:2]))
     for half in range(2):
         left, gated = (
-            jnp.concatenate(pair, axis=0) for pair in zip(own_blocks[half], block(1, next_keys, next_norm, half))
+            jnp.concatenate(pair, axis=0) for pair in zip(inner_blocks[half], block(*outer_set, half))
         )
         grad = dot(left, keys, TN)
         if half == 0:
             gout[: 2 * hid] = grad.astype(BF16)
-            for i in range(2 * per):
+
+            @pl.when(leaf)
+            def _():
+                for i in range(SKIP):
+                    skew(i).start()
+
+            @pl.when(center)
+            def _():
+                for i in range(SKIP):
+                    aside(i).start()
+
+            for i in range(SKIP, 2 * per):
                 aside(i).start()
         else:
             gfull[: 2 * hid] = grad
+
+            @pl.when(leaf)
+            def _():
+                for i in range(SKIP):
+                    gsum[rows(i)] = gfull[rows(i)].astype(BF16)
+                    early(i).start()
+
         grad = dot(gated, steps, TN)
         if half == 0:
             gout[2 * hid:] = grad.astype(BF16)
@@ -444,11 +479,18 @@
         cnt[3] = cnt[2] + cnt[3]
         cnt_down.start()
 
+    wold[0:hid] = wft[:, 2 * hid:3 * hid].astype(F32).T
+    wold[hid:2 * hid] = wft[:, 3 * hid:].astype(F32).T
+    wold[2 * hid:] = ws[hid:].astype(F32)
     ss[0, 2:3] = jnp.sum(wold[:hid] * wold[:hid], axis=0, keepdims=True)
     ss[0, 3:4] = jnp.sum(wold[hid:2 * hid] * wold[hid:2 * hid], axis=0, keepdims=True)
     second_old = wold[2 * hid:]
     second_size = jnp.sqrt(jnp.sum(second_old * second_old, axis=-1, keepdims=True) + 1e-06)
 
+    def here(i, count):
+        at = gin.at[pl.ds(0, count * piece)]
+        return remote(at, at, view_send.at[2], side_recv.at[i], "view", inner)
+
     def rise(i, target, receives):
         return remote(gsum.at[rows(i)], target.at[rows(i)], view_send.at[2], receives.at[i], "view", inner)
 
@@ -456,14 +498,17 @@
         return remote(gtot.at[rows(i)], gtot.at[rows(i)], view_send.at[3], total_recv.at[i], "view", outer)
 
     def lift(i):
+        if i < SKIP:
+            return
         aside(i).wait_recv()
         gsum[rows(i)] = (gfull[rows(i)] + gside[rows(i)].astype(F32)).astype(BF16)
-        rise(i, gin, out_recv).start()
+        rise(i, gin, side_recv).start()
 
     def join(i):
-        aside(i).wait_recv()
+        here(i, 3 if i < SKIP else 2).wait_recv()
         partial = gfull[rows(i)] + gside[rows(i)].astype(F32)
-        rise(i, gin, out_recv).wait_recv()
+        if i < SKIP:
+            partial = partial + gslant[rows(i)].astype(F32)
         gsum[rows(i)] = (partial + gin[rows(i)].astype(F32)).astype(BF16)
         rise(i, gtot, total_recv).start()
 
@@ -508,32 +553,45 @@
         size = jnp.sqrt(jnp.sum(raised * raised, axis=-1, keepdims=True) + 1e-06)
         news[0, rows(i)] = (raised * (second_size[at:at + piece] / size)).astype(BF16)
 
-    groups = [(0, per), (per, 2 * per), (2 * per, 3 * per - 2), (3 * per - 2, 3 * per - 1), (3 * per - 1, 3 * per)]
+    tail = per // 8
+    groups = [(0, per), (per, 2 * per), (2 * per, 3 * per - 2 * tail), (3 * per - 2 * tail, 3 * per - tail), (3 * per - tail, 3 * per)]
 
     def span(group):
         return pl.ds(group[0] * piece, (group[1] - group[0]) * piece)
 
+    def group_of(i):
+        return [g for g, group in enumerate(groups) if group[0] <= i < group[1]][0]
+
     def lend(i):
-        return remote(news.at[0, rows(i)], news.at[2, rows(i)], row_send.at[5], far_recv.at[i], "row", across)
-
-    def pair(g, slot, receives):
+        return remote(news.at[0, rows(i)], news.at[2, rows(i)], row_send.at[5], far_recv.at[min(group_of(i), 3)], "row", across)
+
+    def lend_over(i):
+        return remote(news.at[0, rows(i)], news.at[3, rows(i)], row_send.at[5 + nr], on_recv.at[1], "row", flip(me, 3))
+
+    def pair(g, slot, receives, sends=5):
         return remote(
-            news.at[slot, span(groups[g])], news.at[slot + 1, span(groups[g])], row_send.at[5], receives.at[g], "row", partner
+            news.at[slot, span(groups[g])], news.at[slot + 1, span(groups[g])], row_send.at[sends], receives.at[g // 2 if g < 2 else 1], "row", partner
         )
 
-    def relay(i):
-        lend(i).wait_recv()
-        for g, group in enumerate(groups):
-            if group[1] == i + 1:
-                pair(g, 2, on_recv).start()
+    def parts_here(part, slot, receives):
+        at = pl.ds(part * 2 * hid, (2 - part) * hid)
+        remote(news.at[slot, at], news.at[slot + 1, at], row_send.at[5], receives.at[part], "row", partner).wait_recv()
+
+    def relay(g):
+        remote(
+            news.at[0, span(groups[g])], news.at[2, span(groups[g])], row_send.at[5], far_recv.at[g], "row", across
+        ).wait_recv()
+        pair(g, 2, on_recv, 6 + nr).start()
 
     ss_copies = [
-        remote(ss.at[0], ss.at[d], row_send.at[5 + d], row_recv.at[4 + d], "row", flip(me, d)) for d in range(1, nr)
+        remote(ss.at[0], ss.at[d], row_send.at[5 + d], row_recv.at[2 + d], "row", flip(me, d)) for d in range(1, nr)
     ]
     for i in range(pieces):
         arrive(i)
         square = raise_rows(i)
         lend(i).start()
+        if group_of(i) > 2:
+            lend_over(i).start()
         for g, group in enumerate(groups):
             if group[1] == i + 1:
                 pair(g, 0, near_recv).start()
@@ -545,16 +603,16 @@
                 if m == 1:
                     for copy in ss_copies:
                         copy.start()
-        if i >= HOLD:
-            relay(i - HOLD)
-    for i in range(pieces - HOLD, 2 * per):
-        relay(i)
+    relay(0)
+    relay(1)
     for copy in ss_copies:
         copy.wait_recv()
     sums = ss[0]
     for d in range(1, nr):
         sums = sums + ss[d]
     scales = jnp.sqrt(sums[2:4] + 1e-06) / jnp.sqrt(sums[0:2] + 1e-06)
+    own_keys = keys_of(0, (slice(0, tokens),))
+    own_norm = token_norm(own_keys)
     wide = own_keys.astype(F32)
     scaled = [(wide * scales[m:m + 1]).astype(BF16) for m in range(2)]
 
@@ -564,24 +622,19 @@
         return (first * jax.nn.sigmoid(first) * third).astype(BF16)
 
     applied = [apply(0)]
-    for g in range(2):
-        pair(g, 0, near_recv).wait_recv()
+    parts_here(0, 0, near_recv)
     applied.append(apply(1))
     applied.append(apply(2))
-    for i in range(max(pieces - HOLD, 2 * per), groups[2][1]):
-        relay(i)
-    for g in range(2):
-        pair(g, 2, on_recv).wait_recv()
+    relay(2)
+    parts_here(0, 2, on_recv)
     applied.append(apply(3))
-    for i in range(max(pieces - HOLD, groups[2][1]), pieces):
-        relay(i)
     total = dot(applied[0], news[0, 2 * hid:])
-    for g in range(2, len(groups)):
-        pair(g, 0, near_recv).wait_recv()
+    parts_here(1, 0, near_recv)
     total = total + dot(applied[1], news[1, 2 * hid:])
+    lent = span((groups[3][0], pieces))
+    remote(news.at[0, lent], news.at[2, lent], row_send.at[5], far_recv.at[3], "row", across).wait_recv()
     total = total + dot(applied[2], news[2, 2 * hid:])
-    for g in range(2, len(groups)):
-        pair(g, 2, on_recv).wait_recv()
+    parts_here(1, 2, on_recv)
     total = total + dot(applied[3], news[3, 2 * hid:])
     out_ref[...] = total.astype(BF16)
 
@@ -594,18 +647,21 @@
         down_halo.wait_send()
 
     s_near.wait_send()
-    remote(raw.at[0], raw.at[1], row_send.at[3], row_recv.at[2], "row", partner).wait_send()
-    remote(gout, gside, row_send.at[4], row_recv.at[2], "row", across).wait_send()
-    remote(news.at[pl.ds(0, 3)], news.at[pl.ds(0, 3)], row_send.at[5], row_recv.at[2], "row", partner).wait_send()
+    remote(raw.at[0], raw.at[1], row_send.at[3], row_recv.at[0], "row", partner).wait_send()
+    remote(gout, gside, row_send.at[4], row_recv.at[0], "row", across).wait_send()
+    sent = pl.ds(0, 3 * hid - (pieces - groups[3][0]) * piece)
+    remote(news.at[pl.ds(0, 2)], news.at[pl.ds(0, 2)], row_send.at[5], row_recv.at[0], "row", partner).wait_send()
+    remote(news.at[2, sent], news.at[3, sent], row_send.at[6 + nr], row_recv.at[0], "row", partner).wait_send()
+    remote(news.at[0, lent], news.at[3, lent], row_send.at[5 + nr], row_recv.at[0], "row", partner).wait_send()
     for copy in ss_copies:
         copy.wait_send()
-    remote(gsum, gin, view_send.at[2], row_recv.at[2], "view", inner).wait_send()
+    remote(gsum, gin, view_send.at[2], row_recv.at[0], "view", inner).wait_send()
     cnt_up.wait_send()
 
     @pl.when(center)
     def _():
         cnt_down.wait_send()
-        remote(gtot, gtot, view_send.at[3], row_recv.at[2], "view", outer).wait_send()
+        remote(gtot, gtot, view_send.at[3], row_recv.at[0], "view", outer).wait_send()
 
 
 def fused_step(
@@ -641,6 +697,7 @@
             pltpu.VMEM((4, 8, 128), F32),
             pltpu.VMEM((3 * hid, width), BF16),
             pltpu.VMEM((3 * hid, width), BF16),
+            pltpu.VMEM((3 * hid, width), BF16),
             pltpu.VMEM((3 * hid, width), F32),
             pltpu.VMEM((3 * hid, width), BF16),
             pltpu.VMEM((3 * hid, width), BF16),
@@ -649,16 +706,16 @@
             pltpu.VMEM((nr, 3 * hid, width), BF16),
             pltpu.VMEM((nr, 4, width), F32),
             pltpu.SemaphoreType.DMA((9,)),
-            pltpu.SemaphoreType.DMA((5 + nr,)),
-            pltpu.SemaphoreType.DMA((4 + nr,)),
+            pltpu.SemaphoreType.DMA((7 + nr,)),
+            pltpu.SemaphoreType.DMA((2 + nr,)),
+            pltpu.SemaphoreType.DMA((2, 2)),
             pltpu.SemaphoreType.DMA((2,)),
             pltpu.SemaphoreType.DMA((4,)),
             pltpu.SemaphoreType.DMA((pieces,)),
             pltpu.SemaphoreType.DMA((pieces,)),
-            pltpu.SemaphoreType.DMA((pieces,)),
-            pltpu.SemaphoreType.DMA((5,)),
-            pltpu.SemaphoreType.DMA((pieces,)),
-            pltpu.SemaphoreType.DMA((5,)),
+            pltpu.SemaphoreType.DMA((2,)),
+            pltpu.SemaphoreType.DMA((4,)),
+            pltpu.SemaphoreType.DMA((2,)),
         ],
         compiler_params=pltpu.CompilerParams(collective_id=0, has_side_effects=True),
     )(

time: 34.5 us -> 32.7 us (0.948)
  Pallas kernels: 33.1 us -> 31.2 us
    pallas_call x1, Pallas kernels: 33.1 us -> 31.2 us  [fused_step(): pl.pallas_call(functools.partial(step_kernel, nr, nz, cols), out_shape=pl...]
where the time goes in v3:
time: 32.7 us; the launch traced here: 32.6 us
  Pallas kernels  31.2 us (95%)
  local copies, waits for them, and re-layouts  0.66 us (2%)
  between operations  0.66 us (2%)
    pallas_call x1, Pallas kernels, fused_step(): pl.pallas_call(functools.partial(step_kernel, nr, nz, cols), out_shape=pl...  31.2 us
    unnamed x1, local copies, waits for them, and re-layouts  0.66 us

profile of v3, /device:TPU:1, one launch (start us, length us, event | category | flops | bytes accessed | tf_op | source)
XLA Modules:
  0.0 32.6 jit_solution(2187214580020462778)
XLA Ops:
  0.7 31.2 %shard_map.100 = bf16[128,512]{1,0:T(8,128)(2,1)S(1)} custom-call(bf16[128,512]{1,0:T(8,128)(2,1)} %bitcast.13, bf16[128,512]{1,0:T(8,128)(2,1)} %bitcast.14, bf16[128,512]{1,0:T(8,128)(2,1)} %bitcast.15, bf16[128,512]{1,0:T(8,128)(2,1)} %bitcast.16, f32[1,128]{1,0:T(1,128)} %bitcast.17, s32[8]{0:T(128)} %reach_hbm.1, s32[1]{0:T(128)S(6)} %copy.13.count_hbm, ...), custom_call_target="tpu_custom_call" | custom-call | tf_op jit(solution)/shard_map/pallas_call | solution.py:680
  31.9 0.7 %copy.12 = bf16[1,8,16,512]{3,2,1,0:T(8,128)(2,1)} copy(bf16[1,8,16,512]{3,2,1,0:T(8,128)(2,1)S(1)} %bitcast.9) | data formatting | bytes 262144

commit v4 on v3

--- a/solution.py
+++ b/solution.py
@@ -13,7 +13,8 @@
 HALO = 2
 PER = 8
 SKIP = 4
-LAGS = (9, 9)
+DIRECT = 2
+LAGS = (9, 8)
 LEADS = (24, 24)
 MESH = pl.DeviceIdType.MESH
 BF16 = jnp.bfloat16
@@ -229,7 +230,7 @@
         pl.semaphore_signal(barrier, inc=1, device_id={"view": outer}, device_id_type=MESH)
 
     loads = [
-        pltpu.make_async_copy(source, target, load_sem.at[min(i, 7) if i < 11 else 8])
+        pltpu.make_async_copy(source, target, load_sem.at[max(min(i, 7) if i < 11 else 8, 1) - 1])
         for i, (source, target) in enumerate((
             (k_hbm, kv_ref.at[0]), (v_hbm, kv_ref.at[1]), (count_hbm, count_ref), (reach_hbm, reach_ref),
             (t_hbm, t_ref), (rates_hbm, rates_ref), (q_hbm, q_ref),
@@ -322,8 +323,8 @@
     )
     root = 1.0 / math.sqrt(ATT_HD)
     spans = [slice(h * ATT_HD, (h + 1) * ATT_HD) for h in range(heads)]
-    for load in loads[:2] + loads[6:7]:
-        load.wait()
+    pltpu.make_async_copy(kv_ref, kv_ref, load_sem.at[0]).wait()
+    loads[6].wait()
     inside = slice(edge, tokens - edge)
     ends = (slice(0, edge), slice(tokens - edge, tokens))
 
@@ -331,7 +332,7 @@
         return jnp.concatenate([value[e] for e in ends], axis=0)
 
     def pass_keys(at, receives):
-        return remote(raw.at[0, :, at], raw.at[1, :, at], row_send.at[3], receives, "row", partner)
+        return remote(raw.at[0, :, at], raw.at[1, :, at], row_send.at[2], receives, "row", partner)
 
     near = []
     for h, hs in enumerate(spans):
@@ -344,8 +345,8 @@
         near.append((outer_rows(top), outer_rows(total), outer_rows(mix), outer_rows(q_ref.at[:, hs])))
     middle = pass_keys(pl.ds(edge, tokens - 2 * edge), k_recv.at[0])
     middle.start()
-    pltpu.make_async_copy(wft, wft, load_sem.at[7]).wait()
-    pltpu.make_async_copy(ws, ws, load_sem.at[8]).wait()
+    pltpu.make_async_copy(wft, wft, load_sem.at[6]).wait()
+    pltpu.make_async_copy(ws, ws, load_sem.at[7]).wait()
     def halo_here(i):
         @pl.when(has_below)
         def _():
@@ -433,17 +434,16 @@
         cnt[2] = cnt[0] + cnt[1]
         cnt_mid.start()
 
+    inner_left, inner_gated = inner_blocks[0]
+    gfull[: 2 * hid] = dot(inner_left, inner_set[0], TN)
+    gfull[2 * hid:] = dot(inner_gated, inner_set[1], TN)
     pass_keys(pl.ds(0, 2 * edge), k_recv.at[1]).wait_recv()
     outer_set = token_set(ends)
-    keys, steps = (jnp.concatenate(pair, axis=0) for pair in zip(inner_set[:2], outer_set[:2]))
-    for half in range(2):
-        left, gated = (
-            jnp.concatenate(pair, axis=0) for pair in zip(inner_blocks[half], block(*outer_set, half))
-        )
-        grad = dot(left, keys, TN)
-        if half == 0:
-            gout[: 2 * hid] = grad.astype(BF16)
-
+    left, gated = block(*outer_set, 0)
+    for m in range(2):
+        at = slice(m * hid, (m + 1) * hid)
+        gout[at] = (gfull[at] + dot(left[:, at], outer_set[0], TN)).astype(BF16)
+        if m == 0:
             @pl.when(leaf)
             def _():
                 for i in range(SKIP):
@@ -454,24 +454,22 @@
                 for i in range(SKIP):
                     aside(i).start()
 
-            for i in range(SKIP, 2 * per):
-                aside(i).start()
-        else:
-            gfull[: 2 * hid] = grad
-
-            @pl.when(leaf)
-            def _():
-                for i in range(SKIP):
-                    gsum[rows(i)] = gfull[rows(i)].astype(BF16)
-                    early(i).start()
-
-        grad = dot(gated, steps, TN)
-        if half == 0:
-            gout[2 * hid:] = grad.astype(BF16)
-            for i in range(2 * per, 3 * per):
-                aside(i).start()
-        else:
-            gfull[2 * hid:] = grad
+        for i in range(SKIP if m == 0 else per, (m + 1) * per):
+            aside(i).start()
+    gout[2 * hid:] = (gfull[2 * hid:] + dot(gated, outer_set[1], TN)).astype(BF16)
+    for i in range(2 * per, 3 * per):
+        aside(i).start()
+    keys, steps = (jnp.concatenate(pair, axis=0) for pair in zip(inner_set[:2], outer_set[:2]))
+    left, gated = (jnp.concatenate(pair, axis=0) for pair in zip(inner_blocks[1], block(*outer_set, 1)))
+    gfull[: 2 * hid] = dot(left, keys, TN)
+
+    @pl.when(leaf)
+    def _():
+        for i in range(SKIP):
+            gsum[rows(i)] = gfull[rows(i)].astype(BF16)
+            early(i).start()
+
+    gfull[2 * hid:] = dot(gated, steps, TN)
 
     @pl.when(center)
     def _():
@@ -553,8 +551,7 @@
         size = jnp.sqrt(jnp.sum(raised * raised, axis=-1, keepdims=True) + 1e-06)
         news[0, rows(i)] = (raised * (second_size[at:at + piece] / size)).astype(BF16)
 
-    tail = per // 8
-    groups = [(0, per), (per, 2 * per), (2 * per, 3 * per - 2 * tail), (3 * per - 2 * tail, 3 * per - tail), (3 * per - tail, 3 * per)]
+    groups = [(0, per), (per, 2 * per), (2 * per, 3 * per - DIRECT), (3 * per - DIRECT, 3 * per)]
 
     def span(group):
         return pl.ds(group[0] * piece, (group[1] - group[0]) * piece)
@@ -563,28 +560,28 @@
         return [g for g, group in enumerate(groups) if group[0] <= i < group[1]][0]
 
     def lend(i):
-        return remote(news.at[0, rows(i)], news.at[2, rows(i)], row_send.at[5], far_recv.at[min(group_of(i), 3)], "row", across)
+        return remote(news.at[0, rows(i)], news.at[2, rows(i)], row_send.at[4], far_recv.at[min(group_of(i), 3)], "row", across)
 
     def lend_over(i):
-        return remote(news.at[0, rows(i)], news.at[3, rows(i)], row_send.at[5 + nr], on_recv.at[1], "row", flip(me, 3))
-
-    def pair(g, slot, receives, sends=5):
+        return remote(news.at[0, rows(i)], news.at[3, rows(i)], row_send.at[4], on_recv.at[1], "row", flip(me, 3))
+
+    def pair(g, slot, receives, sends=4):
         return remote(
             news.at[slot, span(groups[g])], news.at[slot + 1, span(groups[g])], row_send.at[sends], receives.at[g // 2 if g < 2 else 1], "row", partner
         )
 
     def parts_here(part, slot, receives):
         at = pl.ds(part * 2 * hid, (2 - part) * hid)
-        remote(news.at[slot, at], news.at[slot + 1, at], row_send.at[5], receives.at[part], "row", partner).wait_recv()
+        remote(news.at[slot, at], news.at[slot + 1, at], row_send.at[4], receives.at[part], "row", partner).wait_recv()
 
     def relay(g):
         remote(
-            news.at[0, span(groups[g])], news.at[2, span(groups[g])], row_send.at[5], far_recv.at[g], "row", across
+            news.at[0, span(groups[g])], news.at[2, span(groups[g])], row_send.at[4], far_recv.at[g], "row", across
         ).wait_recv()
-        pair(g, 2, on_recv, 6 + nr).start()
+        pair(g, 2, on_recv).start()
 
     ss_copies = [
-        remote(ss.at[0], ss.at[d], row_send.at[5 + d], row_recv.at[2 + d], "row", flip(me, d)) for d in range(1, nr)
+        remote(ss.at[0], ss.at[d], row_send.at[3], row_recv.at[3], "row", flip(me, d)) for d in range(1, nr)
     ]
     for i in range(pieces):
         arrive(i)
@@ -605,8 +602,7 @@
                         copy.start()
     relay(0)
     relay(1)
-    for copy in ss_copies:
-        copy.wait_recv()
+    remote(ss.at[pl.ds(0, nr - 1)], ss.at[pl.ds(1, nr - 1)], row_send.at[3], row_recv.at[3], "row", partner).wait_recv()
     sums = ss[0]
     for d in range(1, nr):
         sums = sums + ss[d]
@@ -632,7 +628,7 @@
     parts_here(1, 0, near_recv)
     total = total + dot(applied[1], news[1, 2 * hid:])
     lent = span((groups[3][0], pieces))
-    remote(news.at[0, lent], news.at[2, lent], row_send.at[5], far_recv.at[3], "row", across).wait_recv()
+    remote(news.at[0, lent], news.at[2, lent], row_send.at[4], far_recv.at[3], "row", across).wait_recv()
     total = total + dot(applied[2], news[2, 2 * hid:])
     parts_here(1, 2, on_recv)
     total = total + dot(applied[3], news[3, 2 * hid:])
@@ -646,15 +642,9 @@
     def _():
         down_halo.wait_send()
 
-    s_near.wait_send()
-    remote(raw.at[0], raw.at[1], row_send.at[3], row_recv.at[0], "row", partner).wait_send()
-    remote(gout, gside, row_send.at[4], row_recv.at[0], "row", across).wait_send()
-    sent = pl.ds(0, 3 * hid - (pieces - groups[3][0]) * piece)
-    remote(news.at[pl.ds(0, 2)], news.at[pl.ds(0, 2)], row_send.at[5], row_recv.at[0], "row", partner).wait_send()
-    remote(news.at[2, sent], news.at[3, sent], row_send.at[6 + nr], row_recv.at[0], "row", partner).wait_send()
-    remote(news.at[0, lent], news.at[3, lent], row_send.at[5 + nr], row_recv.at[0], "row", partner).wait_send()
-    for copy in ss_copies:
-        copy.wait_send()
+    remote(kv_ref, kv_ref, row_send.at[2], row_recv.at[0], "row", partner).wait_send()
+    remote(news, news, row_send.at[4], row_recv.at[0], "row", partner).wait_send()
+    remote(ss.at[pl.ds(0, nr - 1)], ss.at[pl.ds(1, nr - 1)], row_send.at[3], row_recv.at[3], "row", partner).wait_send()
     remote(gsum, gin, view_send.at[2], row_recv.at[0], "view", inner).wait_send()
     cnt_up.wait_send()
 
@@ -705,9 +695,9 @@
             pltpu.VMEM((3 * hid, width), F32),
             pltpu.VMEM((nr, 3 * hid, width), BF16),
             pltpu.VMEM((nr, 4, width), F32),
-            pltpu.SemaphoreType.DMA((9,)),
-            pltpu.SemaphoreType.DMA((7 + nr,)),
-            pltpu.SemaphoreType.DMA((2 + nr,)),
+            pltpu.SemaphoreType.DMA((8,)),
+            pltpu.SemaphoreType.DMA((5,)),
+            pltpu.SemaphoreType.DMA((4,)),
             pltpu.SemaphoreType.DMA((2, 2)),
             pltpu.SemaphoreType.DMA((2,)),
             pltpu.SemaphoreType.DMA((4,)),

time: 32.7 us -> 32.6 us (level)
  no operation moved by 1% of the time
where the time goes in v4:
time: 32.6 us; the launch traced here: 32.4 us
  Pallas kernels  31.1 us (95%)
  local copies, waits for them, and re-layouts  0.66 us (2%)
  between operations  0.66 us (2%)
    pallas_call x1, Pallas kernels, fused_step(): pl.pallas_call(functools.partial(step_kernel, nr, nz, cols), out_shape=pl...  31.1 us
    unnamed x1, local copies, waits for them, and re-layouts  0.66 us

profile of v4, /device:TPU:1, one launch (start us, length us, event | category | flops | bytes accessed | tf_op | source)
XLA Modules:
  0.0 32.4 jit_solution(10377190234118406421)
XLA Ops:
  0.7 31.1 %shard_map.100 = bf16[128,512]{1,0:T(8,128)(2,1)S(1)} custom-call(bf16[128,512]{1,0:T(8,128)(2,1)} %bitcast.13, bf16[128,512]{1,0:T(8,128)(2,1)} %bitcast.14, bf16[128,512]{1,0:T(8,128)(2,1)} %bitcast.15, bf16[128,512]{1,0:T(8,128)(2,1)} %bitcast.16, f32[1,128]{1,0:T(1,128)} %bitcast.17, s32[8]{0:T(128)} %reach_hbm.1, s32[1]{0:T(128)S(6)} %copy.13.count_hbm, ...), custom_call_target="tpu_custom_call" | custom-call | tf_op jit(solution)/shard_map/pallas_call | solution.py:670
  31.8 0.7 %copy.12 = bf16[1,8,16,512]{3,2,1,0:T(8,128)(2,1)} copy(bf16[1,8,16,512]{3,2,1,0:T(8,128)(2,1)S(1)} %bitcast.9) | data formatting | bytes 262144

commit v5 on v4

--- a/solution.py
+++ b/solution.py
@@ -12,7 +12,7 @@
 ATT_HD = 128
 HALO = 2
 PER = 8
-SKIP = 4
+SKIP = 3
 DIRECT = 2
 LAGS = (9, 8)
 LEADS = (24, 24)
@@ -390,28 +390,38 @@
         steps = jnp.concatenate([sall[d, at] for d in range(2) for at in rows_at], axis=0)
         return keys, steps, token_norm(keys)
 
+    def attend_edges():
+        halo_here(0)
+        partly = []
+        for h, hs in enumerate(spans):
+            near_top, near_sum, near_out, queries = near[h]
+            far = jnp.where(far_ok, dot(queries, halo[0, :, hs], NT) * root, -1e30)
+            top = jnp.maximum(near_top, jnp.max(far, axis=-1, keepdims=True))
+            power = jnp.exp(far - top)
+            keep = jnp.exp(near_top - top)
+            inverse = 1.0 / (keep * near_sum + jnp.sum(power, axis=-1, keepdims=True))
+            partly.append((power.astype(BF16), keep * near_out, inverse))
+        halo_here(1)
+        for h, hs in enumerate(spans):
+            power, kept, inverse = partly[h]
+            mix = ((kept + dot(power, halo[1, :, hs])) * inverse).astype(BF16)
+            raw[0, h, ends[0]] = mix[:edge]
+            raw[0, h, ends[1]] = mix[edge:]
+        for e in ends:
+            pass_keys(pl.ds(e.start, edge), k_recv.at[1]).start()
+
+    @pl.when(~(has_above & has_below))
+    def _():
+        attend_edges()
+
     s_near.wait_recv()
     middle.wait_recv()
     inner_set = token_set((inside,))
     inner_blocks = [block(*inner_set, half) for half in range(2)]
-    halo_here(0)
-    partly = []
-    for h, hs in enumerate(spans):
-        near_top, near_sum, near_out, queries = near[h]
-        far = jnp.where(far_ok, dot(queries, halo[0, :, hs], NT) * root, -1e30)
-        top = jnp.maximum(near_top, jnp.max(far, axis=-1, keepdims=True))
-        power = jnp.exp(far - top)
-        keep = jnp.exp(near_top - top)
-        inverse = 1.0 / (keep * near_sum + jnp.sum(power, axis=-1, keepdims=True))
-        partly.append((power.astype(BF16), keep * near_out, inverse))
-    halo_here(1)
-    for h, hs in enumerate(spans):
-        power, kept, inverse = partly[h]
-        mix = ((kept + dot(power, halo[1, :, hs])) * inverse).astype(BF16)
-        raw[0, h, ends[0]] = mix[:edge]
-        raw[0, h, ends[1]] = mix[edge:]
-    for e in ends:
-        pass_keys(pl.ds(e.start, edge), k_recv.at[1]).start()
+
+    @pl.when(has_above & has_below)
+    def _():
+        attend_edges()
 
     def rows(i):
         return pl.ds(i * piece, piece)

time: 32.6 us -> 32.2 us (0.988)
  Pallas kernels: 31.1 us -> 30.7 us
    pallas_call x1, Pallas kernels: 31.1 us -> 30.7 us  [fused_step(): pl.pallas_call(functools.partial(step_kernel, nr, nz, cols), out_shape=pl...]
where the time goes in v5:
time: 32.2 us; the launch traced here: 32.1 us
  Pallas kernels  30.7 us (95%)
  local copies, waits for them, and re-layouts  0.66 us (2%)
  between operations  0.66 us (2%)
    pallas_call x1, Pallas kernels, fused_step(): pl.pallas_call(functools.partial(step_kernel, nr, nz, cols), out_shape=pl...  30.7 us
    unnamed x1, local copies, waits for them, and re-layouts  0.66 us

profile of v5, /device:TPU:1, one launch (start us, length us, event | category | flops | bytes accessed | tf_op | source)
XLA Modules:
  0.0 32.1 jit_solution(5984190719224928184)
XLA Ops:
  0.7 30.7 %shard_map.100 = bf16[128,512]{1,0:T(8,128)(2,1)S(1)} custom-call(bf16[128,512]{1,0:T(8,128)(2,1)} %bitcast.13, bf16[128,512]{1,0:T(8,128)(2,1)} %bitcast.14, bf16[128,512]{1,0:T(8,128)(2,1)} %bitcast.15, bf16[128,512]{1,0:T(8,128)(2,1)} %bitcast.16, f32[1,128]{1,0:T(1,128)} %bitcast.17, s32[8]{0:T(128)} %reach_hbm.1, s32[1]{0:T(128)S(6)} %copy.13.count_hbm, ...), custom_call_target="tpu_custom_call" | custom-call | tf_op jit(solution)/shard_map/pallas_call | solution.py:680
  31.4 0.7 %copy.12 = bf16[1,8,16,512]{3,2,1,0:T(8,128)(2,1)} copy(bf16[1,8,16,512]{3,2,1,0:T(8,128)(2,1)S(1)} %bitcast.9) | data formatting | bytes 262144

commit v6 on v5

--- a/solution.py
+++ b/solution.py
@@ -410,7 +410,7 @@
         for e in ends:
             pass_keys(pl.ds(e.start, edge), k_recv.at[1]).start()
 
-    @pl.when(~(has_above & has_below))
+    @pl.when(~(has_above & has_below) | (me < nr // 2))
     def _():
         attend_edges()
 
@@ -419,7 +419,7 @@
     inner_set = token_set((inside,))
     inner_blocks = [block(*inner_set, half) for half in range(2)]
 
-    @pl.when(has_above & has_below)
+    @pl.when(has_above & has_below & (me >= nr // 2))
     def _():
         attend_edges()
 

time: 32.2 us -> 32.2 us (level)
  no operation moved by 1% of the time
where the time goes in v6:
time: 32.2 us; the launch traced here: 32.1 us
  Pallas kernels  30.8 us (96%)
  local copies, waits for them, and re-layouts  0.66 us (2%)
  between operations  0.66 us (2%)
    pallas_call x1, Pallas kernels, fused_step(): pl.pallas_call(functools.partial(step_kernel, nr, nz, cols), out_shape=pl...  30.8 us
    unnamed x1, local copies, waits for them, and re-layouts  0.66 us

profile of v6, /device:TPU:1, one launch (start us, length us, event | category | flops | bytes accessed | tf_op | source)
XLA Modules:
  0.0 32.1 jit_solution(8349577658527174477)
XLA Ops:
  0.7 30.8 %shard_map.100 = bf16[128,512]{1,0:T(8,128)(2,1)S(1)} custom-call(bf16[128,512]{1,0:T(8,128)(2,1)} %bitcast.13, bf16[128,512]{1,0:T(8,128)(2,1)} %bitcast.14, bf16[128,512]{1,0:T(8,128)(2,1)} %bitcast.15, bf16[128,512]{1,0:T(8,128)(2,1)} %bitcast.16, f32[1,128]{1,0:T(1,128)} %bitcast.17, s32[8]{0:T(128)} %reach_hbm.1, s32[1]{0:T(128)S(6)} %copy.13.count_hbm, ...), custom_call_target="tpu_custom_call" | custom-call | tf_op jit(solution)/shard_map/pallas_call | solution.py:680
  31.4 0.7 %copy.12 = bf16[1,8,16,512]{3,2,1,0:T(8,128)(2,1)} copy(bf16[1,8,16,512]{3,2,1,0:T(8,128)(2,1)S(1)} %bitcast.9) | data formatting | bytes 262144
